TPU v7x, 512 devices: a whole 4x8x8 slice. The times are simulated.
512 devices in a mesh: dp: 16 (over x_lo, y), expert: 32 (over x_hi, z, core).
Axes of the slice: x: 4 (x_hi: 2, x_lo: 2; x = x_hi * 2 + x_lo), y: 8, z: 8, core: 2. Of those that a mesh axis runs over, the one named last changes fastest.
Arguments:
- tokens: bfloat16 [65536, 3584], P(('dp', 'expert')), may hold values from -6 to 6
- grad_out: bfloat16 [65536, 3584], P(('dp', 'expert')), may hold values from -1.5 to 1.5
- route: int32 [16, 32, 32, 1], P('dp', 'expert'), may hold values from 0 to 127
- gates: bfloat16 [16, 32, 32, 1], P('dp', 'expert'), may hold values from 0.099609375 to 1
- w_gate: bfloat16 [32, 3584, 768], P('expert', 'dp'), may hold values from -0.09375 to 0.09375
- w_up: bfloat16 [32, 3584, 768], P('expert', 'dp'), may hold values from -0.09375 to 0.09375
- w_down: bfloat16 [32, 768, 3584], P('expert', None, 'dp'), may hold values from -0.21875 to 0.21875
Outputs:
- grad_tokens: bfloat16 [65536, 3584], P(('dp', 'expert'))
- grad_w_gate: bfloat16 [32, 3584, 768], P('expert', 'dp')
- grad_w_up: bfloat16 [32, 3584, 768], P('expert', 'dp')
- grad_w_down: bfloat16 [32, 768, 3584], P('expert', None, 'dp')
- grad_gates: float32 [16, 32, 32, 1], P('dp', 'expert')
Inputs may be any that keep to these rules, and one draw needn't show every extreme that they name: route[i, j, e, s] is the position, among the 128 tokens of the device at dp index i and expert index j, of the token that expert e takes in slot s from that device; a token may be taken by several experts or slots.
All inputs are finite; a program needn't handle non-finite values.
Results may differ from a plain program's by a relative error of at most 0.017.
Values may be sent and summed in bfloat16 or wider, within the bound.
A program may use at most 64 MiB of HBM per device.

v0:
```python
import jax
import jax.numpy as jnp
from jax import lax
from jax.sharding import PartitionSpec as P


def contract_last(left, right):
    return lax.dot_general(
        left, right, (((1,), (1,)), ((), ())), preferred_element_type=jnp.float32
    )


def contract_first(left, right):
    return lax.dot_general(
        left, right, (((0,), (0,)), ((), ())), preferred_element_type=jnp.float32
    )


def local(tokens, grad_out, route, gates, w_gate, w_up, w_down):
    n_dp = lax.axis_size("dp")
    n_ex = lax.axis_size("expert")
    experts = route.shape[2]
    slots = route.shape[3]
    width = tokens.shape[1]
    piece = width // n_dp
    capacity = n_ex * slots
    rows = n_dp * capacity
    wg = w_gate[0]
    wu = w_up[0]
    wd = w_down[0]
    own_start = lax.axis_index("dp") * capacity
    picks = route.reshape(experts * slots)
    picked_x = jnp.take(tokens, picks, axis=0).reshape(experts, 1, slots, width)
    picked_dy = jnp.take(grad_out, picks, axis=0).reshape(experts, 1, slots, width)
    gate_cols = jnp.broadcast_to(gates.reshape(experts, 1, slots, 1), (experts, 1, slots, n_dp))
    x_in = lax.all_to_all(
        lax.all_to_all(picked_x, "dp", split_axis=3, concat_axis=1, tiled=True),
        "expert",
        split_axis=0,
        concat_axis=2,
        tiled=True,
    )
    x_rows = x_in.reshape(rows, piece)
    gate_pre, up_pre = lax.psum(
        (
            jnp.dot(x_rows, wg, preferred_element_type=jnp.float32),
            jnp.dot(x_rows, wu, preferred_element_type=jnp.float32),
        ),
        "dp",
    )
    hidden_all = (jax.nn.silu(gate_pre) * up_pre).astype(jnp.bfloat16)
    out_rows = jnp.dot(hidden_all, wd, preferred_element_type=jnp.float32).astype(jnp.bfloat16)
    dy_in, g_in = (
        lax.all_to_all(
            lax.all_to_all(picked_dy, "dp", split_axis=3, concat_axis=1, tiled=True),
            "expert",
            split_axis=0,
            concat_axis=2,
            tiled=True,
        ),
        lax.all_to_all(
            lax.all_to_all(gate_cols, "dp", split_axis=3, concat_axis=1, tiled=True),
            "expert",
            split_axis=0,
            concat_axis=2,
            tiled=True,
        ),
    )
    dy_rows = dy_in.reshape(rows, piece)
    gate_rows = g_in.reshape(rows, 1)
    weighted = (gate_rows.astype(jnp.float32) * dy_rows.astype(jnp.float32)).astype(jnp.bfloat16)
    returned = lax.all_to_all(
        lax.all_to_all(
            out_rows.reshape(1, n_dp, capacity, piece),
            "dp",
            split_axis=1,
            concat_axis=3,
            tiled=True,
        ),
        "expert",
        split_axis=2,
        concat_axis=0,
        tiled=True,
    )
    grad_gates = jnp.sum(
        picked_dy.astype(jnp.float32) * returned.astype(jnp.float32), axis=3
    ).reshape(gates.shape)
    grad_own = lax.psum_scatter(contract_last(weighted, wd), "dp", scatter_dimension=0, tiled=True)
    gate_own = lax.dynamic_slice_in_dim(gate_pre, own_start, capacity, 0)
    up_own = lax.dynamic_slice_in_dim(up_pre, own_start, capacity, 0)
    sig = jax.nn.sigmoid(gate_own)
    gate_share = (grad_own * up_own * sig * (1.0 + gate_own * (1.0 - sig))).astype(jnp.bfloat16)
    up_share = (grad_own * gate_own * sig).astype(jnp.bfloat16)
    grad_gate_pre, grad_up_pre = (
        lax.all_gather(gate_share, "dp", axis=0, tiled=True),
        lax.all_gather(up_share, "dp", axis=0, tiled=True),
    )
    grad_rows = (contract_last(grad_gate_pre, wg) + contract_last(grad_up_pre, wu)).astype(
        jnp.bfloat16
    )
    grad_wg = contract_first(x_rows, grad_gate_pre).astype(jnp.bfloat16)[None]
    grad_wu = contract_first(x_rows, grad_up_pre).astype(jnp.bfloat16)[None]
    grad_wd = contract_first(hidden_all, weighted).astype(jnp.bfloat16)[None]
    back = lax.all_to_all(
        lax.all_to_all(
            grad_rows.reshape(1, n_dp, capacity, piece),
            "dp",
            split_axis=1,
            concat_axis=3,
            tiled=True,
        ),
        "expert",
        split_axis=2,
        concat_axis=0,
        tiled=True,
    )
    flat = back.reshape(experts * slots, width).astype(jnp.float32)
    grad_tokens = (
        jnp.zeros((tokens.shape[0], width), jnp.float32).at[picks].add(flat).astype(jnp.bfloat16)
    )
    return (grad_tokens, grad_wg, grad_wu, grad_wd, grad_gates)


def solution(mesh):
    return jax.shard_map(
        local,
        mesh=mesh,
        in_specs=(
            P(("dp", "expert"), None),
            P(("dp", "expert"), None),
            P("dp", "expert", None, None),
            P("dp", "expert", None, None),
            P("expert", "dp", None),
            P("expert", "dp", None),
            P("expert", None, "dp"),
        ),
        out_specs=(
            P(("dp", "expert"), None),
            P("expert", "dp", None),
            P("expert", "dp", None),
            P("expert", None, "dp"),
            P("dp", "expert", None, None),
        ),
        check_vma=False,
    )
```

profile of v0, /device:TPU:1, one launch (start us, length us, event | category | flops | bytes accessed | tf_op | source)
XLA Modules:
  0.0 458.3 jit_solution(1260753636977080706)
XLA Ops:
  13.2 20.6 %reduce.3 = bf16[3584,32]{1,0:T(8,128)(2,1)} reduce(bf16[3584,1,1,32]{3,2,1,0:T(2,128)(2,1)S(1)} %bitcast.118, bf16[]{:T(256)} %broadcast.35), dimensions={1,2}, to_apply=%bitcast.98.reduce_sub_computation | reduce | bytes 458754
  36.1 16.2 %all_to_all.125 = bf16[16,2,3584]{2,1,0:T(2,128)(2,1)S(1)} all-to-all(bf16[16,2,3584]{2,1,0:T(2,128)(2,1)S(1)} %reshape.183), channel_id=1, replica_groups=mesh['dp'=16,'expert'=32] {'dp'}, dimensions={0} | all-to-all | bytes 458752 | tf_op jit(solution)/shard_map/all_to_all | solution.py:37
  55.5 28.7 %all_to_all.126 = bf16[32,16,1,224]{3,1,2,0:T(8,128)(2,1)S(1)} all-to-all(bf16[32,16,1,224]{3,1,2,0:T(8,128)(2,1)S(1)} %bitcast.132), channel_id=1, replica_groups=mesh['dp'=16,'expert'=32] {'expert'}, dimensions={0} | all-to-all | bytes 458752 | tf_op jit(solution)/shard_map/all_to_all | solution.py:36
  88.6 4.1 all-to-all-start
  95.1 20.6 %reduce.2 = bf16[3584,32]{1,0:T(8,128)(2,1)} reduce(bf16[3584,1,1,32]{3,2,1,0:T(2,128)(2,1)S(1)} %bitcast.120, bf16[]{:T(256)} %broadcast.35), dimensions={1,2}, to_apply=%bitcast.96.reduce_sub_computation | reduce | bytes 458754
  115.8 2.8 reshape.181
  118.6 7.5 %all-to-all-start.2 = ((bf16[16,2,3584]{2,1,0:T(2,128)(2,1)}), bf16[16,2,3584]{2,1,0:T(2,128)(2,1)S(1)}, u32[]{:S(2)}, u32[]{:S(2)}) async-start(bf16[16,2,3584]{2,1,0:T(2,128)(2,1)} %reshape.181), calls=%async_computation.2 | async-start | bytes 458752 | tf_op jit(solution)/shard_map/all_to_all | solution.py:55
  126.9 7.6 %all-to-all-done.2 = bf16[16,2,3584]{2,1,0:T(2,128)(2,1)S(1)} async-done(((bf16[16,2,3584]{2,1,0:T(2,128)(2,1)}), bf16[16,2,3584]{2,1,0:T(2,128)(2,1)S(1)}, u32[]{:S(2)}, u32[]{:S(2)}) %all-to-all-start.2) | async-done | bytes 229408 | tf_op jit(solution)/shard_map/all_to_all | solution.py:55
  134.5 8.9 %all-to-all-start.1 = ((bf16[32,16,1,1]{1,3,2,0:T(2,128)(2,1)}), bf16[32,16,1,1]{1,3,2,0:T(2,128)(2,1)S(1)}, u32[]{:S(2)}, u32[]{:S(2)}) async-start(bf16[32,16,1,1]{1,3,2,0:T(2,128)(2,1)} %copy.41), calls=%async_computation.1 | async-start | bytes 32768 | tf_op jit(solution)/shard_map/all_to_all | solution.py:61
  147.4 5.3 %all-to-all-done.1 = bf16[32,16,1,1]{1,3,2,0:T(2,128)(2,1)S(1)} async-done(((bf16[32,16,1,1]{1,3,2,0:T(2,128)(2,1)}), bf16[32,16,1,1]{1,3,2,0:T(2,128)(2,1)S(1)}, u32[]{:S(2)}, u32[]{:S(2)}) %all-to-all-start.1) | async-done | bytes 1056 | tf_op jit(solution)/shard_map/all_to_all | solution.py:61
  152.7 4.5 all-to-all-start.3
  157.3 13.3 %all-to-all-done.3 = bf16[32,16,1,224]{3,1,2,0:T(8,128)(2,1)S(1)} async-done(((bf16[32,16,1,224]{3,1,2,0:T(8,128)(2,1)}), bf16[32,16,1,224]{3,1,2,0:T(8,128)(2,1)S(1)}, u32[]{:S(2)}, u32[]{:S(2)}) %all-to-all-start.3) | async-done | bytes 229408 | tf_op jit(solution)/shard_map/all_to_all | solution.py:54
  172.4 54.4 %all-reduce.3.cloned.1.call-done = (f32[512,768]{1,0:T(8,128)}, f32[512,768]{1,0:T(8,128)}) async-done(((f32[512,768]{1,0:T(8,128)}, f32[512,768]{1,0:T(8,128)}), (f32[512,768]{1,0:T(8,128)}, f32[512,768]{1,0:T(8,128)})) %all-reduce.3.cloned.1.call-update) | async-done | bytes 3145744 | tf_op jit(solution)/shard_map/psum | solution.py:44
  230.5 4.2 all-to-all-start.8
  234.7 66.5 %reduce-scatter.2.cloned.1.call-done = f32[32,768]{1,0:T(8,128)} async-done(((f32[512,768]{1,0:T(8,128)}), f32[32,768]{1,0:T(8,128)}) %reduce-scatter.2.cloned.1.call-update) | async-done | bytes 98320 | tf_op jit(solution)/shard_map/reduce_scatter | solution.py:88
  302.2 29.9 %all_gather.7 = bf16[512,768]{1,0:T(8,128)(2,1)S(1)} all-gather(bf16[32,768]{1,0:T(8,128)(2,1)S(1)} %get-tuple-element.8), channel_id=1, replica_groups=mesh['dp'=16,'expert'=32] {'dp'}, dimensions={0}, use_global_device_ids=true | all-gather | bytes 835584 | tf_op jit(solution)/shard_map/all_gather | solution.py:96
  332.1 27.8 %all_gather.6 = bf16[512,768]{1,0:T(8,128)(2,1)S(1)} all-gather(bf16[32,768]{1,0:T(8,128)(2,1)S(1)} %get-tuple-element.9), channel_id=1, replica_groups=mesh['dp'=16,'expert'=32] {'dp'}, dimensions={0}, use_global_device_ids=true | all-gather | bytes 835584 | tf_op jit(solution)/shard_map/all_gather | solution.py:95
  364.2 4.4 all-to-all-start.6
  375.3 3.6 reduce.5
  380.6 35.9 %all-to-all-start.9 = ((bf16[32,2,1792]{2,1,0:T(2,128)(2,1)}), bf16[32,2,1792]{2,1,0:T(2,128)(2,1)}, u32[]{:S(2)}, u32[]{:S(2)}) async-start(bf16[32,2,1792]{2,1,0:T(2,128)(2,1)} %reshape.187), calls=%async_computation.10 | async-start | bytes 458752 | tf_op jit(solution)/shard_map/all_to_all | solution.py:72
  421.5 2.7 reduce.4
  425.8 3.0 all-to-all-done.9
  428.9 6.8 %all-to-all-start.7 = ((bf16[32,2,1792]{2,1,0:T(2,128)(2,1)}), bf16[32,2,1792]{2,1,0:T(2,128)(2,1)S(1)}, u32[]{:S(2)}, u32[]{:S(2)}) async-start(bf16[32,2,1792]{2,1,0:T(2,128)(2,1)} %reshape.185), calls=%async_computation.8 | async-start | bytes 458752 | tf_op jit(solution)/shard_map/all_to_all | solution.py:104
  440.4 7.7 %all-to-all-done.7 = bf16[32,2,1792]{2,1,0:T(2,128)(2,1)S(1)} async-done(((bf16[32,2,1792]{2,1,0:T(2,128)(2,1)}), bf16[32,2,1792]{2,1,0:T(2,128)(2,1)S(1)}, u32[]{:S(2)}, u32[]{:S(2)}) %all-to-all-start.7) | async-done | bytes 229408 | tf_op jit(solution)/shard_map/all_to_all | solution.py:104
  (87 shorter events, 56.7 us)
Async XLA Ops:
  7.2 1.5 copy-start
  7.2 2.2 copy-start.1
  7.2 219.7 %all-reduce.3.cloned.1.call-start = ((), (), s32[]{:S(2)}) async-start(), calls=%async_computation.12 | async-start | bytes 6291456 | tf_op jit(solution)/shard_map/psum | solution.py:44
  8.0 2.1 copy-start.10
  9.4 0.8 copy-start.3
  53.2 31.0 %copy-start.8 = (bf16[1,224,768]{2,1,0:T(8,128)(2,1)S(1)}, bf16[1,224,768]{2,1,0:T(8,128)(2,1)}, u32[]{:S(2)}) copy-start(bf16[1,224,768]{2,1,0:T(8,128)(2,1)} %param.13) | copy-start | bytes 1032196
  55.5 30.3 %copy-start.5 = (bf16[1,224,768]{2,1,0:T(8,128)(2,1)S(1)}, bf16[1,224,768]{2,1,0:T(8,128)(2,1)}, u32[]{:S(2)}) copy-start(bf16[1,224,768]{2,1,0:T(8,128)(2,1)} %param.14) | copy-start | bytes 1032196
  87.3 0.7 copy-start.12
  88.6 30.0 %all-to-all-start = ((bf16[32,1,1,16]{0,2,1,3:T(2,128)(2,1)}), bf16[32,1,1,16]{0,2,1,3:T(2,128)(2,1)S(1)}, u32[]{:S(2)}, u32[]{:S(2)}) async-start(bf16[32,1,1,16]{0,2,1,3:T(2,128)(2,1)} %broadcast_in_dim.31), calls=%async_computation | async-start | bytes 16384 | tf_op jit(solution)/shard_map/all_to_all | solution.py:62
  118.6 15.9 %all-to-all-start.2 = ((bf16[16,2,3584]{2,1,0:T(2,128)(2,1)}), bf16[16,2,3584]{2,1,0:T(2,128)(2,1)S(1)}, u32[]{:S(2)}, u32[]{:S(2)}) async-start(bf16[16,2,3584]{2,1,0:T(2,128)(2,1)} %reshape.181), calls=%async_computation.2 | async-start | bytes 458752 | tf_op jit(solution)/shard_map/all_to_all | solution.py:55
  134.5 18.2 %all-to-all-start.1 = ((bf16[32,16,1,1]{1,3,2,0:T(2,128)(2,1)}), bf16[32,16,1,1]{1,3,2,0:T(2,128)(2,1)S(1)}, u32[]{:S(2)}, u32[]{:S(2)}) async-start(bf16[32,16,1,1]{1,3,2,0:T(2,128)(2,1)} %copy.41), calls=%async_computation.1 | async-start | bytes 32768 | tf_op jit(solution)/shard_map/all_to_all | solution.py:61
  146.3 24.6 %copy-start.7 = (bf16[1,768,224]{1,2,0:T(8,128)(2,1)S(1)}, bf16[1,768,224]{1,2,0:T(8,128)(2,1)}, u32[]{:S(2)}) copy-start(bf16[1,768,224]{1,2,0:T(8,128)(2,1)} %param.15) | copy-start | bytes 1032196
  152.7 17.9 %all-to-all-start.3 = ((bf16[32,16,1,224]{3,1,2,0:T(8,128)(2,1)}), bf16[32,16,1,224]{3,1,2,0:T(8,128)(2,1)S(1)}, u32[]{:S(2)}, u32[]{:S(2)}) async-start(bf16[32,16,1,224]{3,1,2,0:T(8,128)(2,1)} %bitcast.8), calls=%async_computation.3 | async-start | bytes 524288 | tf_op jit(solution)/shard_map/all_to_all | solution.py:54
  157.2 143.9 %reduce-scatter.2.cloned.1.call-start = ((), (), s32[]{:S(2)}) async-start(), calls=%async_computation.11 | async-start | bytes 1671168 | tf_op jit(solution)/shard_map/reduce_scatter | solution.py:88
  170.6 1.8 copy-start.2
  230.5 133.7 %all-to-all-start.8 = ((bf16[1,16,32,224]{3,2,0,1:T(8,128)(2,1)}), bf16[1,16,32,224]{3,2,0,1:T(8,128)(2,1)}, u32[]{:S(2)}, u32[]{:S(2)}) async-start(bf16[1,16,32,224]{3,2,0,1:T(8,128)(2,1)} %bitcast.31), calls=%async_computation.9 | async-start | bytes 524288 | tf_op jit(solution)/shard_map/all_to_all | solution.py:73
  302.2 59.1 %copy-start.6 = (bf16[1,224,768]{2,1,0:T(8,128)(2,1)S(1)}, bf16[1,224,768]{2,1,0:T(8,128)(2,1)}, u32[]{:S(2)}) copy-start(bf16[1,224,768]{2,1,0:T(8,128)(2,1)} %param.14) | copy-start | bytes 1032196
  364.2 16.4 %all-to-all-start.6 = ((bf16[1,16,32,224]{3,2,0,1:T(8,128)(2,1)}), bf16[1,16,32,224]{3,2,0,1:T(8,128)(2,1)}, u32[]{:S(2)}, u32[]{:S(2)}) async-start(bf16[1,16,32,224]{3,2,0,1:T(8,128)(2,1)} %bitcast.131), calls=%async_computation.7 | async-start | bytes 524288 | tf_op jit(solution)/shard_map/all_to_all | solution.py:105
  380.6 48.3 %all-to-all-start.9 = ((bf16[32,2,1792]{2,1,0:T(2,128)(2,1)}), bf16[32,2,1792]{2,1,0:T(2,128)(2,1)}, u32[]{:S(2)}, u32[]{:S(2)}) async-start(bf16[32,2,1792]{2,1,0:T(2,128)(2,1)} %reshape.187), calls=%async_computation.10 | async-start | bytes 458752 | tf_op jit(solution)/shard_map/all_to_all | solution.py:72
  421.4 15.3 %copy-start.9 = (bf16[512,224]{1,0:T(8,128)(2,1)S(1)}, bf16[512,224]{1,0:T(8,128)(2,1)}, u32[]{:S(2)}) copy-start(bf16[512,224]{1,0:T(8,128)(2,1)} %fusion.6) | copy-start | bytes 688132
  428.9 19.2 %all-to-all-start.7 = ((bf16[32,2,1792]{2,1,0:T(2,128)(2,1)}), bf16[32,2,1792]{2,1,0:T(2,128)(2,1)S(1)}, u32[]{:S(2)}, u32[]{:S(2)}) async-start(bf16[32,2,1792]{2,1,0:T(2,128)(2,1)} %reshape.185), calls=%async_computation.8 | async-start | bytes 458752 | tf_op jit(solution)/shard_map/all_to_all | solution.py:104
  435.7 3.9 copy-start.4
  435.7 3.9 copy-start.11
Sparse Core Ops, SparseCore 0:
  87.5 139.3 all-reduce.2
  229.7 71.3 reduce-scatter.1
where the time goes:
time: 460 us; the launch traced here: 458 us
  waiting for transfers between devices  158 us (34%)
  blocking collectives  103 us (22%)
  starting transfers between devices  76.4 us (17%)
  other arithmetic  59.8 us (13%)
  local copies, waits for them, and re-layouts  36.4 us (8%)
  between operations  14.5 us (3%)
  matrix products  10.8 us (2%)
    reduce_scatter x1, waiting for transfers between devices, local(): lax.psum_scatter(contract_last(weighted, wd), 'dp', scatter_dimension=0,...  66.5 us
    psum x1, waiting for transfers between devices, local(): lax.psum((jnp.dot(x_rows, wg, preferred_element_type=jnp.float32), jnp.do...  54.4 us
    unnamed x4, other arithmetic  47.6 us
    all_to_all x1, starting transfers between devices, local(): lax.all_to_all(lax.all_to_all(out_rows.reshape(1, n_dp, capacity, piece),...  35.9 us
    all_gather x1, blocking collectives, local(): lax.all_gather(up_share, 'dp', axis=0, tiled=True)  29.9 us
    all_to_all x1, blocking collectives, local(): lax.all_to_all(lax.all_to_all(picked_x, 'dp', split_axis=3, concat_axis=1...  28.7 us
    all_gather x1, blocking collectives, local(): lax.all_gather(gate_share, 'dp', axis=0, tiled=True)  27.8 us
    all_to_all x1, blocking collectives, local(): lax.all_to_all(picked_x, 'dp', split_axis=3, concat_axis=1, tiled=True)  16.2 us
  transfers between devices with their start and end apart: 10, of which 7 were waited for; matrix products, arithmetic and copies ran while one was open for 14% of the time, Pallas kernels for 0%

commit v1 on v0

v1 whole, which is shorter than its diff:
```python
import functools

import jax
import jax.numpy as jnp
from jax import lax
from jax.experimental import pallas as pl
from jax.experimental.pallas import tpu as pltpu
from jax.sharding import PartitionSpec as P

NX = 2
F32 = jnp.float32
BF16 = jnp.bfloat16


def dot(a, b, ca=1, cb=0):
    return lax.dot_general(a, b, (((ca,), (cb,)), ((), ())), preferred_element_type=F32)


def kernel(
    cfg,
    tokens, grad_out, route, gates, wg, wu, wd,
    gt_out, gwg_out, gwu_out, gwd_out, gg_out,
    tok_v, dyo_v, wg_v, wu_v, wd_v, wide, perm, a1, r1, a2, r2, part, acc, arm,
    xsend, xrecv, q_all, own_gg, a3, r3, a4, r4, gw_v, gwd_v, gt_v,
    load_sem, s1_sem, r1_sem, s2_sem, r2_sem, as_sem, ar_sem, xs_sem, xr_sem,
    qs_sem, qr_sem, qxs_sem, qxr_sem, s3_sem, r3_sem, s4_sem, r4_sem, out_sem,
):
    n_dp, n_ex, piece, width, hid = cfg
    ny = n_dp // NX
    n_rows = n_dp * n_ex
    d_model = n_dp * piece
    cap = n_ex
    half = 3 * hid // 2
    long_arm = ny // 2
    win = width + 128

    me = lax.axis_index("dp")
    ex = lax.axis_index("expert")
    xl = me // ny
    y = lax.rem(me, ny)
    pair = (1 - xl) * ny + y

    def y_of(off):
        return lax.rem(y + off + 2 * ny, ny)

    def rows(k, n):
        return pl.ds(pl.multiple_of(k * n, n), n)

    barrier = pltpu.get_barrier_semaphore()

    def greet_dp(s, c):
        pl.semaphore_signal(barrier, inc=1, device_id={"dp": lax.rem(me + s, n_dp)})
        return c

    def greet_ex(s, c):
        pl.semaphore_signal(barrier, inc=1, device_id={"expert": lax.rem(ex + s, n_ex)})
        return c

    lax.fori_loop(1, n_dp, greet_dp, 0)
    lax.fori_loop(1, n_ex, greet_ex, 0)

    loads = [
        pltpu.make_async_copy(src, dst, load_sem.at[n])
        for n, (src, dst) in enumerate(
            [(tokens, tok_v), (grad_out, dyo_v), (wg, wg_v), (wu, wu_v), (wd, wd_v)]
        )
    ]
    for load in loads:
        load.start()

    r_id = lax.broadcasted_iota(jnp.int32, (n_rows, n_rows), 0)
    c_id = lax.broadcasted_iota(jnp.int32, (n_rows, n_rows), 1)
    perm[...] = jnp.where(c_id == lax.rem(r_id, n_dp) * n_ex + r_id // n_dp, 1.0, 0.0).astype(BF16)

    tok_dev = tokens.shape[0]
    t_id = lax.broadcasted_iota(jnp.int32, (n_ex, tok_dev), 1)
    pick = jnp.where(t_id == route[...], 1.0, 0.0).astype(BF16)
    gate_own = gates[...].astype(F32)
    lane = lax.broadcasted_iota(jnp.int32, (n_ex, width), 1)

    wide[:, d_model:] = jnp.zeros((n_ex, wide.shape[1] - d_model), F32)

    def gather(q, src):
        wide[:, :d_model] = dot(pick, src[...])
        for d in range(n_dp):
            start = (piece * d) // 128 * 128
            shift = piece * d - start
            v = wide[:, start:start + win]
            if shift:
                v = pltpu.roll(v, win - shift, 1)
            v = v[:, :width]
            pad = jnp.where(lane == piece, gate_own, 0.0) if q == 0 else 0.0
            a1[q, d * n_ex:(d + 1) * n_ex, :] = jnp.where(lane < piece, v, pad).astype(BF16)

    def dp_copy(q, k, slot, src, dst, send, recv):
        return pltpu.make_async_remote_copy(
            src_ref=src.at[q, rows(k, n_ex)],
            dst_ref=dst.at[q, rows(slot, n_ex)],
            send_sem=send.at[q, k],
            recv_sem=recv.at[q, slot],
            device_id={"dp": k},
        )

    def ex_copy(q, k, slot, src, dst, send, recv):
        return pltpu.make_async_remote_copy(
            src_ref=src.at[q, rows(k, n_dp)],
            dst_ref=dst.at[q, rows(slot, n_dp)],
            send_sem=send.at[q, k],
            recv_sem=recv.at[q, slot],
            device_id={"expert": k},
        )

    def exchange(copy, n, mine, size, q, src, dst, send, recv):
        pltpu.make_async_copy(
            src.at[q, rows(mine, size)], dst.at[q, rows(mine, size)], recv.at[q, mine]
        ).start()

        def go(s, c):
            copy(q, lax.rem(mine + s, n), mine, src, dst, send, recv).start()
            return c

        lax.fori_loop(1, n, go, 0)

    def arrive(n, size, q, src, dst, recv):
        def one(k, c):
            pltpu.make_async_copy(
                src.at[q, rows(k, size)], dst.at[q, rows(k, size)], recv.at[q, k]
            ).wait()
            return c

        lax.fori_loop(0, n, one, 0)

    def drain(copy, n, mine, q, src, dst, send, recv):
        def one(s, c):
            copy(q, lax.rem(mine + s, n), mine, src, dst, send, recv).wait_send()
            return c

        lax.fori_loop(1, n, one, 0)

    loads[0].wait()
    gather(0, tok_v)
    pl.semaphore_wait(barrier, n_dp + n_ex - 2)
    exchange(dp_copy, n_dp, me, n_ex, 0, a1, r1, s1_sem, r1_sem)
    loads[1].wait()
    gather(1, dyo_v)
    exchange(dp_copy, n_dp, me, n_ex, 1, a1, r1, s1_sem, r1_sem)
    for q in range(2):
        arrive(n_dp, n_ex, q, a1, r1, r1_sem)
        a2[q] = dot(perm[...], r1[q]).astype(BF16)
        exchange(ex_copy, n_ex, ex, n_dp, q, a2, r2, s2_sem, r2_sem)
    for load in loads[2:]:
        load.wait()

    def partial(m, value):
        part[:, :, :, m * hid:(m + 1) * hid] = value.astype(BF16).reshape(NX, ny, cap, hid)

    arrive(n_ex, n_dp, 0, a2, r2, r2_sem)
    partial(0, dot(r2[0, :, :piece], wg_v[...]))
    partial(1, dot(r2[0, :, :piece], wu_v[...]))
    arrive(n_ex, n_dp, 1, a2, r2, r2_sem)
    partial(2, dot(r2[1, :, :piece], wd_v[...], 1, 1))

    def arm_len(g, s):
        return long_arm if g == s else long_arm - 1

    def cols(g):
        return slice(g * half, (g + 1) * half)

    def arm_copy(g, s, h):
        sign = 1 if s == 0 else -1
        n = arm_len(g, s)
        owner = y_of(sign * (n - h))
        src = part.at[:, owner, :, cols(g)] if h == 0 else acc.at[s, h, :, :, cols(g)]
        return pltpu.make_async_remote_copy(
            src_ref=src,
            dst_ref=arm.at[s, h, :, :, cols(g)],
            send_sem=as_sem.at[s, h, g],
            recv_sem=ar_sem.at[s, h, g],
            device_id={"dp": xl * ny + y_of(sign)},
        )

    lanes = [(g, s) for g in range(2) for s in range(2)]
    for h in range(long_arm):
        for g, s in lanes:
            sign = 1 if s == 0 else -1
            n = arm_len(g, s)
            if h >= n:
                continue
            if h > 0:
                arm_copy(g, s, h - 1).wait_recv()
                mine = part[:, y_of(sign * (n - h)), :, cols(g)].astype(F32)
                got = arm[s, h - 1, :, :, cols(g)].astype(F32)
                acc[s, h, :, :, cols(g)] = (mine + got).astype(BF16)
            arm_copy(g, s, h).start()

    def total(side, g):
        out = part[side, y, :, cols(g)].astype(F32)
        for s in range(2):
            out = out + arm[s, arm_len(g, s) - 1, side, :, cols(g)].astype(F32)
        return out

    def x_copy(g):
        return pltpu.make_async_remote_copy(
            src_ref=xsend.at[:, cols(g)],
            dst_ref=xrecv.at[:, cols(g)],
            send_sem=xs_sem.at[g],
            recv_sem=xr_sem.at[g],
            device_id={"dp": pair},
        )

    for g in range(2):
        for s in range(2):
            arm_copy(g, s, arm_len(g, s) - 1).wait_recv()
        xsend[:, cols(g)] = total(1 - xl, g).astype(BF16)
        x_copy(g).start()
    pieces = []
    for g in range(2):
        x_copy(g).wait_recv()
        pieces.append(total(xl, g) + xrecv[:, cols(g)].astype(F32))
    full = jnp.concatenate(pieces, axis=1)
    gate_pre = full[:, :hid]
    up_pre = full[:, hid:2 * hid]
    base = full[:, 2 * hid:]
    gate_rows = r2[0, rows(me, cap), :].astype(F32)
    wl = lax.broadcasted_iota(jnp.int32, (cap, width), 1)
    gate_w = jnp.sum(jnp.where(wl == piece, gate_rows, 0.0), axis=1, keepdims=True)
    sig = 1.0 / (1.0 + jnp.exp(-gate_pre))
    act = gate_pre * sig
    hidden = act * up_pre
    grad_hidden = gate_w * base
    own_gg[...] = jnp.broadcast_to(
        jnp.sum(hidden * base, axis=1, keepdims=True), own_gg.shape
    )
    mine = q_all.at[xl, y]
    mine[:, :hid] = (gate_w * hidden).astype(BF16)
    mine[:, hid:2 * hid] = (
        grad_hidden * up_pre * sig * (1.0 + gate_pre * (1.0 - sig))
    ).astype(BF16)
    mine[:, 2 * hid:] = (grad_hidden * act).astype(BF16)

    def q_pair():
        return pltpu.make_async_remote_copy(
            src_ref=q_all.at[xl, y],
            dst_ref=q_all.at[xl, y],
            send_sem=qxs_sem.at[0],
            recv_sem=qxr_sem.at[0],
            device_id={"dp": pair},
        )

    def q_copy(c, s, h):
        sign = 1 if s == 0 else -1
        side = xl if c == 0 else 1 - xl
        block = q_all.at[side, y_of(-sign * h)]
        if h == long_arm - 1:
            block = block.at[:, cols(s)]
        return pltpu.make_async_remote_copy(
            src_ref=block,
            dst_ref=block,
            send_sem=qs_sem.at[c, s, h],
            recv_sem=qr_sem.at[c, s, h],
            device_id={"dp": xl * ny + y_of(sign)},
        )

    q_pair().start()
    for h in range(long_arm):
        for c in range(2):
            if h == 0 and c == 1:
                q_pair().wait_recv()
            for s in range(2):
                if h > 0:
                    q_copy(c, s, h - 1).wait_recv()
                q_copy(c, s, h).start()
    for c in range(2):
        for s in range(2):
            q_copy(c, s, long_arm - 1).wait_recv()

    def back(m):
        return q_all[:, :, :, m * hid:(m + 1) * hid].reshape(n_rows, hid)

    a3[0, :, width - 128:] = jnp.zeros((n_rows, 128), BF16)
    a3[0, :, :piece] = (dot(back(1), wg_v[...], 1, 1) + dot(back(2), wu_v[...], 1, 1)).astype(BF16)
    tail = a3[0, rows(me, cap), width - 128:].astype(F32)
    tl = lax.broadcasted_iota(jnp.int32, tail.shape, 1) + (width - 128)
    rest = own_gg[...]
    for n in range(3):
        top = rest.astype(BF16).astype(F32)
        tail = jnp.where(tl == piece + n, top, tail)
        rest = rest - top
    a3[0, rows(me, cap), width - 128:] = tail.astype(BF16)
    exchange(ex_copy, n_ex, ex, n_dp, 0, a3, r3, s3_sem, r3_sem)

    outs = [
        pltpu.make_async_copy(gw_v.at[0], gwg_out, out_sem.at[0]),
        pltpu.make_async_copy(gw_v.at[1], gwu_out, out_sem.at[1]),
        pltpu.make_async_copy(gwd_v, gwd_out, out_sem.at[2]),
        pltpu.make_async_copy(gt_v, gt_out, out_sem.at[3]),
    ]
    gw_v[0] = dot(r2[0, :, :piece], back(1), 0, 0).astype(BF16)
    outs[0].start()
    gw_v[1] = dot(r2[0, :, :piece], back(2), 0, 0).astype(BF16)
    outs[1].start()
    gwd_v[...] = dot(back(0), r2[1, :, :piece], 0, 0).astype(BF16)
    outs[2].start()

    arrive(n_ex, n_dp, 0, a3, r3, r3_sem)
    a4[0] = dot(perm[...], r3[0], 0, 0).astype(BF16)
    exchange(dp_copy, n_dp, me, n_ex, 0, a4, r4, s4_sem, r4_sem)
    wide[...] = jnp.zeros(wide.shape, F32)
    arrive(n_dp, n_ex, 0, a4, r4, r4_sem)
    sums = jnp.zeros((n_ex, width), F32)
    for d in range(n_dp):
        start = (piece * d) // 128 * 128
        shift = piece * d - start
        v = r4[0, d * n_ex:(d + 1) * n_ex, :].astype(F32)
        sums = sums + jnp.where((lane >= piece) & (lane < piece + 3), v, 0.0)
        v = jnp.concatenate([jnp.where(lane < piece, v, 0.0), jnp.zeros((n_ex, 128), F32)], axis=1)
        if shift:
            v = pltpu.roll(v, shift, 1)
        wide[:, start:start + win] += v
    gg_out[...] = jnp.sum(sums, axis=1, keepdims=True)
    gt_v[...] = dot(pick, wide[:, :d_model].astype(BF16), 0, 0).astype(BF16)
    outs[3].start()

    for q in range(2):
        drain(dp_copy, n_dp, me, q, a1, r1, s1_sem, r1_sem)
        drain(ex_copy, n_ex, ex, q, a2, r2, s2_sem, r2_sem)
    for g, s in lanes:
        for h in range(arm_len(g, s)):
            arm_copy(g, s, h).wait_send()
    for g in range(2):
        x_copy(g).wait_send()
    q_pair().wait_send()
    for h in range(long_arm):
        for c in range(2):
            for s in range(2):
                q_copy(c, s, h).wait_send()
    drain(ex_copy, n_ex, ex, 0, a3, r3, s3_sem, r3_sem)
    drain(dp_copy, n_dp, me, 0, a4, r4, s4_sem, r4_sem)
    for out in outs:
        out.wait()


def local(tokens, grad_out, route, gates, w_gate, w_up, w_down):
    n_dp = lax.axis_size("dp")
    n_ex = lax.axis_size("expert")
    piece, hid = w_gate.shape[1:]
    tok_dev, d_model = tokens.shape
    width = (piece + 3 + 127) // 128 * 128
    n_rows = n_dp * n_ex
    ny = n_dp // NX
    arm_n = ny // 2
    cap = n_ex
    dma = pltpu.SemaphoreType.DMA
    any_spec = pl.BlockSpec(memory_space=pl.ANY)
    vmem_spec = pl.BlockSpec(memory_space=pltpu.VMEM)
    outs = pl.pallas_call(
        functools.partial(kernel, (n_dp, n_ex, piece, width, hid)),
        out_shape=(
            jax.ShapeDtypeStruct((tok_dev, d_model), BF16),
            jax.ShapeDtypeStruct((piece, hid), BF16),
            jax.ShapeDtypeStruct((piece, hid), BF16),
            jax.ShapeDtypeStruct((hid, piece), BF16),
            jax.ShapeDtypeStruct((n_ex, 1), F32),
        ),
        in_specs=[any_spec, any_spec, vmem_spec, vmem_spec, any_spec, any_spec, any_spec],
        out_specs=(any_spec, any_spec, any_spec, any_spec, vmem_spec),
        scratch_shapes=[
            pltpu.VMEM((tok_dev, d_model), BF16),
            pltpu.VMEM((tok_dev, d_model), BF16),
            pltpu.VMEM((piece, hid), BF16),
            pltpu.VMEM((piece, hid), BF16),
            pltpu.VMEM((hid, piece), BF16),
            pltpu.VMEM((n_ex, d_model + width + 128), F32),
            pltpu.VMEM((n_rows, n_rows), BF16),
            pltpu.VMEM((2, n_rows, width), BF16),
            pltpu.VMEM((2, n_rows, width), BF16),
            pltpu.VMEM((2, n_rows, width), BF16),
            pltpu.VMEM((2, n_rows, width), BF16),
            pltpu.VMEM((NX, ny, cap, 3 * hid), BF16),
            pltpu.VMEM((2, arm_n, NX, cap, 3 * hid), BF16),
            pltpu.VMEM((2, arm_n, NX, cap, 3 * hid), BF16),
            pltpu.VMEM((cap, 3 * hid), BF16),
            pltpu.VMEM((cap, 3 * hid), BF16),
            pltpu.VMEM((NX, ny, cap, 3 * hid), BF16),
            pltpu.VMEM((cap, 128), F32),
            pltpu.VMEM((1, n_rows, width), BF16),
            pltpu.VMEM((1, n_rows, width), BF16),
            pltpu.VMEM((1, n_rows, width), BF16),
            pltpu.VMEM((1, n_rows, width), BF16),
            pltpu.VMEM((2, piece, hid), BF16),
            pltpu.VMEM((hid, piece), BF16),
            pltpu.VMEM((tok_dev, d_model), BF16),
            dma((5,)),
            dma((2, n_dp)), dma((2, n_dp)),
            dma((2, n_ex)), dma((2, n_ex)),
            dma((2, arm_n, 2)), dma((2, arm_n, 2)),
            dma((2,)), dma((2,)),
            dma((2, 2, arm_n)), dma((2, 2, arm_n)),
            dma((1,)), dma((1,)),
            dma((1, n_ex)), dma((1, n_ex)),
            dma((1, n_dp)), dma((1, n_dp)),
            dma((4,)),
        ],
        compiler_params=pltpu.CompilerParams(
            collective_id=0, has_side_effects=True, vmem_limit_bytes=56 * 1024 * 1024
        ),
        name="moe",
    )(
        tokens,
        grad_out,
        route.reshape(n_ex, 1),
        gates.reshape(n_ex, 1),
        w_gate[0],
        w_up[0],
        w_down[0],
    )
    gt, gwg, gwu, gwd, gg = outs
    return gt, gwg[None], gwu[None], gwd[None], gg.reshape(gates.shape)


def solution(mesh):
    return jax.shard_map(
        local,
        mesh=mesh,
        in_specs=(
            P(("dp", "expert"), None),
            P(("dp", "expert"), None),
            P("dp", "expert", None, None),
            P("dp", "expert", None, None),
            P("expert", "dp", None),
            P("expert", "dp", None),
            P("expert", None, "dp"),
        ),
        out_specs=(
            P(("dp", "expert"), None),
            P("expert", "dp", None),
            P("expert", "dp", None),
            P("expert", None, "dp"),
            P("dp", "expert", None, None),
        ),
        check_vma=False,
    )
```

time: 460 us -> 133 us (0.29)
  waiting for transfers between devices: 158 us -> 0 us
  Pallas kernels: 0 us -> 121 us
  blocking collectives: 103 us -> 0 us
  starting transfers between devices: 76.4 us -> 0 us
  other arithmetic: 59.8 us -> 1.35 us
  local copies, waits for them, and re-layouts: 36.4 us -> 9.86 us
  between operations: 14.5 us -> 0.65 us
  matrix products: 10.8 us -> 0 us
    pallas_call x0 -> x1, Pallas kernels: none -> 121 us  [local(): pl.pallas_call(functools.partial(kernel, (n_dp, n_ex, piece, width, hid))...]
    all_to_all x8 -> x0, starting transfers between devices: 76.3 us -> none  [the longest x1 35.9 us: local(): lax.all_to_all(lax.all_to_all(out_rows.reshape(1, n_dp, capacity, piece),...]
    reduce_scatter x1 -> x0, waiting for transfers between devices: 66.5 us -> none  [local(): lax.psum_scatter(contract_last(weighted, wd), 'dp', scatter_dimension=0,...]
    all_gather x2 -> x0, blocking collectives: 57.7 us -> none  [the longest x1 29.9 us: local(): lax.all_gather(up_share, 'dp', axis=0, tiled=True)]
    psum x1 -> x0, waiting for transfers between devices: 54.4 us -> none  [local(): lax.psum((jnp.dot(x_rows, wg, preferred_element_type=jnp.float32), jnp.do...]
    unnamed x4 -> x0, other arithmetic: 47.6 us -> none
    all_to_all x2 -> x0, blocking collectives: 44.8 us -> none  [the longest x1 28.7 us: local(): lax.all_to_all(lax.all_to_all(picked_x, 'dp', split_axis=3, concat_axis=1...]
    all_to_all x8 -> x0, waiting for transfers between devices: 37 us -> none  [the longest x1 13.3 us: local(): lax.all_to_all(lax.all_to_all(picked_dy, 'dp', split_axis=3, concat_axis=...]
  transfers between devices with their start and end apart: 10 -> 0, of which waited for: 7 -> 0; matrix products, arithmetic and copies ran while one was open for 14% -> 0% of each run, Pallas kernels for 0% -> 0%
where the time goes in v1:
time: 133 us; the launch traced here: 132 us
  Pallas kernels  121 us (91%)
  local copies, waits for them, and re-layouts  9.86 us (7%)
  other arithmetic  1.35 us (1%)
    pallas_call x1, Pallas kernels, local(): pl.pallas_call(functools.partial(kernel, (n_dp, n_ex, piece, width, hid))...  121 us
    unnamed x13, local copies, waits for them, and re-layouts  8.48 us

profile of v1, /device:TPU:1, one launch (start us, length us, event | category | flops | bytes accessed | tf_op | source)
XLA Modules:
  0.0 132.5 jit_solution(10321668076200235743)
XLA Ops:
  0.6 0.0 copy-start.2
  0.6 0.6 copy-done.2
  1.3 0.0 copy-start.3
  1.3 0.7 copy.18.gates
  2.0 0.0 copy-done.3
  2.0 0.7 copy.17.route
  2.7 1.9 %copy.16 = bf16[1,768,224]{2,1,0:T(8,128)(2,1)} copy(bf16[1,768,224]{1,2,0:T(8,128)(2,1)} %param.13) | data formatting | bytes 688128 | tf_op args[6]
  4.6 120.6 %moe.1 = (bf16[128,3584]{1,0:T(8,128)(2,1)}, bf16[224,768]{1,0:T(8,128)(2,1)}, bf16[224,768]{1,0:T(8,128)(2,1)}, bf16[768,224]{1,0:T(8,128)(2,1)}, f32[32,1]{1,0:T(8,128)}) custom-call(bf16[128,3584]{1,0:T(8,128)(2,1)} %tokens.1, bf16[128,3584]{1,0:T(8,128)(2,1)} %grad_out.1, s32[32,1]{1,0:T(8,128)} %copy.17.route, bf16[32,1]{1,0:T(8,128)(2,1)} %copy.18.gates, ...), custom_call_target="tpu_custom_call" | custom-call | tf_op jit(solution)/shard_map/moe/pallas_call | solution.py:356
  125.2 1.3 %reduce = f32[32]{0:T(128)} reduce(f32[32,1]{1,0:T(8,128)} %get-tuple-element.14, f32[]{:T(128)} %constant.7), dimensions={1}, to_apply=%get-tuple-element.14.reduce_sub_computation | reduce | bytes 260 | tf_op jit(solution)/shard_map/moe/pallas_call | solution.py:356
  126.5 1.9 %copy.19 = bf16[1,768,224]{1,2,0:T(8,128)(2,1)} copy(bf16[1,768,224]{2,1,0:T(8,128)(2,1)} %bitcast.10) | data formatting | bytes 688128
  128.4 0.0 copy-start.1
  128.4 2.2 %copy.23 = bf16[128,3584]{1,0:T(8,128)(2,1)} copy(bf16[128,3584]{1,0:T(8,128)(2,1)} %get-tuple-element.30) | data formatting | bytes 1835008
  130.6 0.0 copy-done.1
  130.6 0.0 copy-start
  130.6 0.7 copy.24
  131.4 0.4 copy-done
  131.7 0.7 copy.25
Async XLA Ops:
  0.6 0.7 copy-start.2
  1.3 0.7 copy-start.3
  128.4 2.2 %copy-start.1 = (bf16[224,768]{1,0:T(8,128)(2,1)S(1)}, bf16[224,768]{1,0:T(8,128)(2,1)}, u32[]{:S(2)}) copy-start(bf16[224,768]{1,0:T(8,128)(2,1)} %get-tuple-element.11) | copy-start | bytes 1032196
  130.6 1.1 copy-start

commit v2 on v1

v2 whole, which is shorter than its diff:
```python
import functools

import jax
import jax.numpy as jnp
from jax import lax
from jax.experimental import pallas as pl
from jax.experimental.pallas import tpu as pltpu
from jax.sharding import PartitionSpec as P

NX = 2
F32 = jnp.float32
BF16 = jnp.bfloat16


def dot(a, b, ca=1, cb=0):
    return lax.dot_general(a, b, (((ca,), (cb,)), ((), ())), preferred_element_type=F32)


def one_hot_rows(route, tok_dev):
    n_ex = route.shape[1]
    t_id = lax.broadcasted_iota(jnp.int32, (tok_dev, n_ex), 0)
    return jnp.where(t_id == jnp.broadcast_to(route, (tok_dev, n_ex)), 1.0, 0.0).astype(BF16)


def kernel(
    cfg,
    tokens, grad_out, route, gates, wg, wu, wd,
    r4, gwg_out, gwu_out, gwd_out,
    tok_v, dyo_v, wg_v, wu_v, wd_v, route_v, gates_v, wide, perm, a1, r1, a2, r2,
    part, xa, arm_a, acc_a, arm_b, acc_b, xsend, xrecv, q_all, own_gg, a3, r3, a4, gw_v,
    load_sem, s1_sem, r1_sem, s2_sem, r2_sem, xas_sem, xar_sem, as_sem, ar_sem, xs_sem, xr_sem,
    qs_sem, qr_sem, qxs_sem, qxr_sem, s3_sem, r3_sem, s4_sem, r4_sem, out_sem,
):
    n_dp, n_ex, piece, width, hid = cfg
    ny = n_dp // NX
    n_rows = n_dp * n_ex
    d_model = n_dp * piece
    cap = n_ex
    hh = hid // 2
    win = width + 128

    me = lax.axis_index("dp")
    ex = lax.axis_index("expert")
    xl = me // ny
    y = lax.rem(me, ny)
    pair = (1 - xl) * ny + y

    def y_of(off):
        return lax.rem(y + off + 2 * ny, ny)

    def y_dev(off):
        return {"dp": xl * ny + y_of(off)}

    def rows(k, n):
        return pl.ds(pl.multiple_of(k * n, n), n)

    barrier = pltpu.get_barrier_semaphore()

    def greet_dp(s, c):
        pl.semaphore_signal(barrier, inc=1, device_id={"dp": lax.rem(me + s, n_dp)})
        return c

    def greet_ex(s, c):
        pl.semaphore_signal(barrier, inc=1, device_id={"expert": lax.rem(ex + s, n_ex)})
        return c

    lax.fori_loop(1, n_ex, greet_ex, 0)
    lax.fori_loop(1, n_dp, greet_dp, 0)

    loads = [
        pltpu.make_async_copy(src, dst, load_sem.at[n])
        for n, (src, dst) in enumerate(
            [
                (route, route_v), (gates, gates_v), (tokens, tok_v), (grad_out, dyo_v),
                (wg, wg_v), (wu, wu_v), (wd, wd_v),
            ]
        )
    ]
    for load in loads:
        load.start()

    lane = lax.broadcasted_iota(jnp.int32, (n_ex, width), 1)
    wide[:, d_model:] = jnp.zeros((n_ex, wide.shape[1] - d_model), F32)
    for load in loads[:3]:
        load.wait()
    pick = one_hot_rows(route_v[...], tok_v.shape[0])
    e_row = lax.broadcasted_iota(jnp.int32, (n_ex, n_ex), 0)
    e_col = lax.broadcasted_iota(jnp.int32, (n_ex, n_ex), 1)
    gate_row = jnp.broadcast_to(gates_v[...].astype(F32), (n_ex, n_ex))
    gate_own = jnp.sum(jnp.where(e_row == e_col, gate_row, 0.0), axis=1, keepdims=True)

    def gather(q, src):
        wide[:, :d_model] = dot(pick, src[...], 0, 0)
        for d in range(n_dp):
            start = (piece * d) // 128 * 128
            shift = piece * d - start
            v = wide[:, start:start + win]
            if shift:
                v = pltpu.roll(v, win - shift, 1)
            v = v[:, :width]
            pad = jnp.where(lane == piece, gate_own, 0.0) if q == 0 else 0.0
            a1[q, d * n_ex:(d + 1) * n_ex, :] = jnp.where(lane < piece, v, pad).astype(BF16)

    class Exchange:
        def __init__(self, axis, q, src, dst, send, recv):
            self.axis = axis
            self.n, self.mine, self.size = (n_dp, me, n_ex) if axis == "dp" else (n_ex, ex, n_dp)
            self.src, self.dst = src.at[q], dst.at[q]
            self.send, self.recv = send.at[q], recv.at[q]

        def start(self):
            own = rows(self.mine, self.size)
            pltpu.make_async_copy(self.src.at[own], self.dst.at[own], self.recv).start()

            def go(s, c):
                k = lax.rem(self.mine + s, self.n)
                pltpu.make_async_remote_copy(
                    src_ref=self.src.at[rows(k, self.size)],
                    dst_ref=self.dst.at[own],
                    send_sem=self.send,
                    recv_sem=self.recv,
                    device_id={self.axis: k},
                ).start()
                return c

            lax.fori_loop(1, self.n, go, 0)

        def arrive(self):
            pltpu.make_async_copy(self.src, self.dst, self.recv).wait()

        def drain(self):
            sent = self.src.at[pl.ds(0, (self.n - 1) * self.size)]
            pltpu.make_async_copy(sent, sent, self.send).wait()

    ex1 = [Exchange("dp", q, a1, r1, s1_sem, r1_sem) for q in range(2)]
    ex2 = [Exchange("expert", q, a2, r2, s2_sem, r2_sem) for q in range(2)]
    ex3 = Exchange("expert", 0, a3, r3, s3_sem, r3_sem)
    ex4 = Exchange("dp", 0, a4, r4, s4_sem, r4_sem)

    gather(0, tok_v)
    pl.semaphore_wait(barrier, n_dp + n_ex - 2)
    ex1[0].start()
    loads[3].wait()
    gather(1, dyo_v)
    ex1[1].start()
    r_id = lax.broadcasted_iota(jnp.int32, (n_rows, n_rows), 0)
    c_id = lax.broadcasted_iota(jnp.int32, (n_rows, n_rows), 1)
    perm[...] = jnp.where(c_id == lax.rem(r_id, n_dp) * n_ex + r_id // n_dp, 1.0, 0.0).astype(BF16)
    for q in range(2):
        ex1[q].arrive()
        a2[q] = dot(perm[...], r1[q]).astype(BF16)
        ex2[q].start()
    for load in loads[4:]:
        load.wait()

    def partial(m, value):
        value = value.astype(BF16)
        for c in range(2):
            part[m, c] = value[:, c * hh:(c + 1) * hh].reshape(NX, ny, cap, hh)

    def arm_len(m, c, s):
        return ny // 2 - (m + c + s) % 2

    def sign(s):
        return 1 - 2 * s

    def xa_copy(m, off):
        block = y_of(off)
        return pltpu.make_async_remote_copy(
            src_ref=part.at[m, 0, 1 - xl, block],
            dst_ref=xa.at[m, block],
            send_sem=xas_sem.at[0],
            recv_sem=xar_sem.at[m, off % ny],
            device_id={"dp": pair},
        )

    far_first = sorted(range(-(ny // 2) + 1, ny // 2 + 1), key=lambda o: -abs(o))

    def xa_send(m):
        for off in far_first:
            xa_copy(m, off).start()

    def arm_copy(m, c, s, h):
        arm, acc = ((arm_a, acc_a), (arm_b, acc_b))[c]
        if c == 1 and h == 0:
            src = part.at[m, 1, :, y_of(sign(s) * arm_len(m, c, s))]
        else:
            src = acc.at[m, s, h]
        return pltpu.make_async_remote_copy(
            src_ref=src,
            dst_ref=arm.at[m, s, h],
            send_sem=as_sem.at[c],
            recv_sem=ar_sem.at[m, c, s, h],
            device_id=y_dev(sign(s)),
        )

    def hop(m, c, h):
        for s in range(2):
            n = arm_len(m, c, s)
            if h >= n:
                continue
            off = sign(s) * (n - h)
            owner = y_of(off)
            if c == 0:
                xa_copy(m, off).wait_recv()
                v = part[m, 0, xl, owner].astype(F32) + xa[m, owner].astype(F32)
                if h > 0:
                    arm_copy(m, c, s, h - 1).wait_recv()
                    v = v + arm_a[m, s, h - 1].astype(F32)
                acc_a[m, s, h] = v.astype(BF16)
            elif h > 0:
                arm_copy(m, c, s, h - 1).wait_recv()
                v = part[m, 1, :, owner].astype(F32) + arm_b[m, s, h - 1].astype(F32)
                acc_b[m, s, h] = v.astype(BF16)
            arm_copy(m, c, s, h).start()

    def x_copy(m):
        return pltpu.make_async_remote_copy(
            src_ref=xsend.at[m],
            dst_ref=xrecv.at[m],
            send_sem=xs_sem.at[0],
            recv_sem=xr_sem.at[m],
            device_id={"dp": pair},
        )

    def b_total(m, side):
        v = part[m, 1, side, y].astype(F32)
        for s in range(2):
            v = v + arm_b[m, s, arm_len(m, 1, s) - 1, side].astype(F32)
        return v

    def b_end(m):
        for s in range(2):
            arm_copy(m, 1, s, arm_len(m, 1, s) - 1).wait_recv()
        xsend[m] = b_total(m, 1 - xl).astype(BF16)
        x_copy(m).start()

    def finish(m):
        xa_copy(m, 0).wait_recv()
        v = part[m, 0, xl, y].astype(F32) + xa[m, y].astype(F32)
        for s in range(2):
            n = arm_len(m, 0, s)
            arm_copy(m, 0, s, n - 1).wait_recv()
            v = v + arm_a[m, s, n - 1].astype(F32)
        x_copy(m).wait_recv()
        return jnp.concatenate([v, b_total(m, xl) + xrecv[m].astype(F32)], axis=1)

    last = ny // 2

    ex2[0].arrive()
    partial(0, dot(r2[0, :, :piece], wg_v[...]))
    xa_send(0)
    hop(0, 1, 0)
    partial(1, dot(r2[0, :, :piece], wu_v[...]))
    xa_send(1)
    hop(1, 1, 0)
    hop(0, 0, 0)
    hop(0, 1, 1)
    ex2[1].arrive()
    partial(2, dot(r2[1, :, :piece], wd_v[...]))
    xa_send(2)
    hop(2, 1, 0)
    for h in range(1, last + 2):
        for m, c, k in (
            (1, 1, h), (1, 0, h - 1), (0, 0, h), (0, 1, h + 1), (2, 1, h), (2, 0, h - 1)
        ):
            if k < last:
                hop(m, c, k)
            elif k == last and c == 1:
                b_end(m)
    gate_pre = finish(0)
    up_pre = finish(1)
    gate_rows = r2[0, rows(me, cap), :].astype(F32)
    wl = lax.broadcasted_iota(jnp.int32, (cap, width), 1)
    gate_w = jnp.sum(jnp.where(wl == piece, gate_rows, 0.0), axis=1, keepdims=True)
    sig = 1.0 / (1.0 + jnp.exp(-gate_pre))
    act = gate_pre * sig
    hidden = act * up_pre
    slope = up_pre * sig * (1.0 + gate_pre * (1.0 - sig))
    base = finish(2)
    grad_hidden = gate_w * base

    def keep(m, value):
        value = value.astype(BF16)
        for c in range(2):
            q_all[m, c, xl, y] = value[:, c * hh:(c + 1) * hh]

    def q_remote(block, send, recv, device):
        return pltpu.make_async_remote_copy(
            src_ref=block, dst_ref=block, send_sem=send, recv_sem=recv, device_id=device
        )

    def q_xb(m):
        return q_remote(q_all.at[m, 1, xl, y], qxs_sem.at[1], qxr_sem.at[m, 1], {"dp": pair})

    def q_xa(m, off):
        block = q_all.at[m, 0, xl, y_of(off)]
        return q_remote(block, qxs_sem.at[0], qxr_sem.at[m, 0], {"dp": pair})

    def q_arm(m, c, s, h):
        owner = y_of(-sign(s) * h)
        block = q_all.at[m, 0, xl, owner] if c == 0 else q_all.at[m, 1, :, owner]
        return q_remote(block, qs_sem.at[c], qr_sem.at[m, c, s, h], y_dev(sign(s)))

    def q_hop(m, c, h):
        if h == 0:
            if c == 0:
                q_xa(m, 0).start()
            else:
                q_xb(m).wait_recv()
        for s in range(2):
            n = arm_len(m, c, s)
            if h > n:
                continue
            if h > 0:
                q_arm(m, c, s, h - 1).wait_recv()
            if h < n:
                q_arm(m, c, s, h).start()
            if c == 0 and h > 0:
                q_xa(m, -sign(s) * h).start()

    def q_end(m):
        side = q_all.at[m, 0, 1 - xl]
        pltpu.make_async_copy(side, side, qxr_sem.at[m, 0]).wait()

    keep(1, grad_hidden * slope)
    q_xb(1).start()
    q_hop(1, 0, 0)
    keep(2, grad_hidden * act)
    q_xb(2).start()
    q_hop(2, 0, 0)
    keep(0, gate_w * hidden)
    q_xb(0).start()
    own_gg[...] = jnp.broadcast_to(jnp.sum(hidden * base, axis=1, keepdims=True), own_gg.shape)
    q_hop(1, 1, 0)
    q_hop(2, 1, 0)
    q_hop(0, 0, 0)
    for h in range(1, last + 1):
        q_hop(1, 0, h)
        q_hop(1, 1, h)
        q_hop(2, 0, h)
        q_hop(2, 1, h)
        q_hop(0, 1, h - 1)
        if h < last:
            q_hop(0, 0, h)
    q_end(1)
    q_end(2)

    def back(m):
        return jnp.concatenate(
            [q_all[m, c].reshape(n_rows, hh) for c in range(2)], axis=1
        )

    a3[0, :, width - 128:] = jnp.zeros((n_rows, 128), BF16)
    a3[0, :, :piece] = (dot(back(1), wg_v[...], 1, 1) + dot(back(2), wu_v[...], 1, 1)).astype(BF16)
    tail = a3[0, rows(me, cap), width - 128:].astype(F32)
    tl = lax.broadcasted_iota(jnp.int32, tail.shape, 1) + (width - 128)
    rest = own_gg[...]
    for n in range(3):
        top = rest.astype(BF16).astype(F32)
        tail = jnp.where(tl == piece + n, top, tail)
        rest = rest - top
    a3[0, rows(me, cap), width - 128:] = tail.astype(BF16)
    ex3.start()

    q_hop(0, 0, last)
    q_hop(0, 1, last)
    outs = [
        pltpu.make_async_copy(gw_v.at[m], dst, out_sem.at[m])
        for m, dst in ((1, gwg_out), (2, gwu_out), (0, gwd_out))
    ]
    gw_v[1] = dot(r2[0, :, :piece], back(1), 0, 0).astype(BF16)
    outs[0].start()
    gw_v[2] = dot(r2[0, :, :piece], back(2), 0, 0).astype(BF16)
    outs[1].start()

    ex3.arrive()
    a4[0] = dot(perm[...], r3[0], 0, 0).astype(BF16)
    ex4.start()
    q_end(0)
    gw_v[0] = dot(r2[1, :, :piece], back(0), 0, 0).astype(BF16)
    outs[2].start()
    ex4.arrive()

    for x in (*ex1, *ex2, ex3, ex4):
        x.drain()

    def sent(ref, sem):
        pltpu.make_async_copy(ref, ref, sem).wait()

    sent(part.at[:, 0, 0], xas_sem.at[0])
    sent(part.at[:, 0, 0, pl.ds(0, ny - 1)], as_sem.at[0])
    sent(part.at[:, 1, :, pl.ds(0, ny - 1)], as_sem.at[1])
    sent(xsend, xs_sem.at[0])
    sent(part.at[:, 0, 0], qxs_sem.at[0])
    sent(xsend, qxs_sem.at[1])
    sent(part.at[:, 0, 0, pl.ds(0, ny - 1)], qs_sem.at[0])
    sent(part.at[:, 1, :, pl.ds(0, ny - 1)], qs_sem.at[1])
    for out in outs:
        out.wait()


def last_kernel(
    cfg, r4, route, gwg, gwu, gwd, gt_out, gg_out, gwg_out, gwu_out, gwd_out,
    r4_v, route_v, gw_v, wide, gt_v, gg_v, in_sem, out_sem,
):
    n_dp, n_ex, piece, width, hid = cfg
    d_model = n_dp * piece
    win = width + 128
    ins = [
        pltpu.make_async_copy(src, dst, in_sem.at[n])
        for n, (src, dst) in enumerate(
            [(r4, r4_v), (route, route_v)]
            + [(src, gw_v.at[m]) for m, src in enumerate((gwg, gwu, gwd))]
        )
    ]
    outs = [
        pltpu.make_async_copy(src, dst, out_sem.at[n])
        for n, (src, dst) in enumerate(
            [(gw_v.at[m], dst) for m, dst in enumerate((gwg_out, gwu_out, gwd_out))]
            + [(gg_v, gg_out), (gt_v, gt_out)]
        )
    ]
    for copy in ins:
        copy.start()
    wide[...] = jnp.zeros(wide.shape, F32)
    ins[0].wait()
    ins[1].wait()
    lane = lax.broadcasted_iota(jnp.int32, (n_ex, width), 1)
    sums = jnp.zeros((n_ex, width), F32)
    for d in range(n_dp):
        start = (piece * d) // 128 * 128
        shift = piece * d - start
        v = r4_v[0, d * n_ex:(d + 1) * n_ex, :].astype(F32)
        sums = sums + jnp.where((lane >= piece) & (lane < piece + 3), v, 0.0)
        v = jnp.concatenate([jnp.where(lane < piece, v, 0.0), jnp.zeros((n_ex, 128), F32)], axis=1)
        if shift:
            v = pltpu.roll(v, shift, 1)
        wide[:, start:start + win] += v
    for n in range(3):
        ins[2 + n].wait()
        outs[n].start()
    e_row = lax.broadcasted_iota(jnp.int32, (n_ex, n_ex), 0)
    e_col = lax.broadcasted_iota(jnp.int32, (n_ex, n_ex), 1)
    column = jnp.broadcast_to(jnp.sum(sums, axis=1, keepdims=True), (n_ex, n_ex))
    gg_v[...] = jnp.sum(jnp.where(e_row == e_col, column, 0.0), axis=0, keepdims=True)
    outs[3].start()
    pick = one_hot_rows(route_v[...], gt_v.shape[0])
    gt_v[...] = dot(pick, wide[:, :d_model].astype(BF16)).astype(BF16)
    outs[4].start()
    for copy in outs:
        copy.wait()


def local(tokens, grad_out, route, gates, w_gate, w_up, w_down):
    n_dp = lax.axis_size("dp")
    n_ex = lax.axis_size("expert")
    piece, hid = w_gate.shape[1:]
    tok_dev, d_model = tokens.shape
    width = (piece + 3 + 127) // 128 * 128
    n_rows = n_dp * n_ex
    ny = n_dp // NX
    hops = ny // 2
    cap = n_ex
    hh = hid // 2
    dma = pltpu.SemaphoreType.DMA
    any_spec = pl.BlockSpec(memory_space=pl.ANY)
    cfg = (n_dp, n_ex, piece, width, hid)
    weights = jax.ShapeDtypeStruct((piece, hid), BF16)
    route_row = route.reshape(1, n_ex)
    wide = pltpu.VMEM((n_ex, d_model + width + 128), F32)
    block = pltpu.VMEM((2, n_rows, width), BF16)
    one_block = pltpu.VMEM((1, n_rows, width), BF16)
    r4, gwg, gwu, gwd = pl.pallas_call(
        functools.partial(kernel, cfg),
        out_shape=(jax.ShapeDtypeStruct((1, n_rows, width), BF16), weights, weights, weights),
        in_specs=[any_spec] * 7,
        out_specs=(any_spec,) * 4,
        scratch_shapes=[
            pltpu.VMEM((tok_dev, d_model), BF16),
            pltpu.VMEM((tok_dev, d_model), BF16),
            pltpu.VMEM((piece, hid), BF16),
            pltpu.VMEM((piece, hid), BF16),
            pltpu.VMEM((piece, hid), BF16),
            pltpu.VMEM((1, n_ex), jnp.int32),
            pltpu.VMEM((1, n_ex), BF16),
            wide,
            pltpu.VMEM((n_rows, n_rows), BF16),
            block, block, block, block,
            pltpu.VMEM((3, 2, NX, ny, cap, hh), BF16),
            pltpu.VMEM((3, ny, cap, hh), BF16),
            pltpu.VMEM((3, 2, hops, cap, hh), BF16),
            pltpu.VMEM((3, 2, hops, cap, hh), BF16),
            pltpu.VMEM((3, 2, hops, NX, cap, hh), BF16),
            pltpu.VMEM((3, 2, hops, NX, cap, hh), BF16),
            pltpu.VMEM((3, cap, hh), BF16),
            pltpu.VMEM((3, cap, hh), BF16),
            pltpu.VMEM((3, 2, NX, ny, cap, hh), BF16),
            pltpu.VMEM((cap, 128), F32),
            one_block, one_block, one_block,
            pltpu.VMEM((3, piece, hid), BF16),
            dma((7,)),
            dma((2,)), dma((2,)),
            dma((2,)), dma((2,)),
            dma((1,)), dma((3, ny)),
            dma((2,)), dma((3, 2, 2, hops)),
            dma((1,)), dma((3,)),
            dma((2,)), dma((3, 2, 2, hops)),
            dma((2,)), dma((3, 2)),
            dma((1,)), dma((1,)),
            dma((1,)), dma((1,)),
            dma((3,)),
        ],
        compiler_params=pltpu.CompilerParams(
            collective_id=0, has_side_effects=True, vmem_limit_bytes=56 * 1024 * 1024
        ),
        name="moe",
    )(
        tokens,
        grad_out,
        route_row,
        gates.reshape(1, n_ex),
        w_gate[0],
        w_up[0],
        jnp.swapaxes(w_down[0], 0, 1),
    )
    gt, gg, gwg, gwu, gwd = pl.pallas_call(
        functools.partial(last_kernel, cfg),
        out_shape=(
            jax.ShapeDtypeStruct((tok_dev, d_model), BF16),
            jax.ShapeDtypeStruct((1, n_ex), F32),
            weights, weights, weights,
        ),
        in_specs=[any_spec] * 5,
        out_specs=(any_spec,) * 5,
        scratch_shapes=[
            pltpu.VMEM((1, n_rows, width), BF16),
            pltpu.VMEM((1, n_ex), jnp.int32),
            pltpu.VMEM((3, piece, hid), BF16),
            wide,
            pltpu.VMEM((tok_dev, d_model), BF16),
            pltpu.VMEM((1, n_ex), F32),
            dma((5,)),
            dma((5,)),
        ],
        compiler_params=pltpu.CompilerParams(vmem_limit_bytes=56 * 1024 * 1024),
        name="scatter",
    )(r4, route_row, gwg, gwu, gwd)
    return (
        gt, gwg[None], gwu[None], jnp.swapaxes(gwd, 0, 1)[None], gg.reshape(gates.shape),
    )


def solution(mesh):
    return jax.shard_map(
        local,
        mesh=mesh,
        in_specs=(
            P(("dp", "expert"), None),
            P(("dp", "expert"), None),
            P("dp", "expert", None, None),
            P("dp", "expert", None, None),
            P("expert", "dp", None),
            P("expert", "dp", None),
            P("expert", None, "dp"),
        ),
        out_specs=(
            P(("dp", "expert"), None),
            P("expert", "dp", None),
            P("expert", "dp", None),
            P("expert", None, "dp"),
            P("dp", "expert", None, None),
        ),
        check_vma=False,
    )
```

time: 133 us -> 105 us (0.79)
  Pallas kernels: 121 us -> 104 us
  local copies, waits for them, and re-layouts: 9.86 us -> 0 us
  other arithmetic: 1.35 us -> 0 us
    pallas_call x1 -> x2, Pallas kernels: 121 us -> 104 us  [the longest x1 101 us: local(): pl.pallas_call(functools.partial(kernel, cfg), out_shape=(jax.ShapeDtypeS...]
    unnamed x13 -> x0, local copies, waits for them, and re-layouts: 8.48 us -> none
    reshape x2 -> x0, local copies, waits for them, and re-layouts: 1.38 us -> none  [the longest x1 0.69 us: local(): gates.reshape(n_ex, 1)]
    pallas_call x1 -> x0, other arithmetic: 1.35 us -> none  [local(): pl.pallas_call(functools.partial(kernel, (n_dp, n_ex, piece, width, hid))...]
where the time goes in v2:
time: 105 us
  Pallas kernels  104 us (99%)
    pallas_call x1, Pallas kernels, local(): pl.pallas_call(functools.partial(kernel, cfg), out_shape=(jax.ShapeDtypeS...  101 us
    pallas_call x1, Pallas kernels, local(): pl.pallas_call(functools.partial(last_kernel, cfg), out_shape=(jax.ShapeD...  2.67 us

profile of v2, /device:TPU:1, one launch (start us, length us, event | category | flops | bytes accessed | tf_op | source)
XLA Modules:
  0.0 104.6 jit_solution(17660694272224955414)
XLA Ops:
  0.6 101.3 %moe.1 = (bf16[1,512,256]{2,1,0:T(8,128)(2,1)}, bf16[224,768]{1,0:T(8,128)(2,1)}, bf16[224,768]{1,0:T(8,128)(2,1)}, bf16[224,768]{1,0:T(8,128)(2,1)}) custom-call(bf16[128,3584]{1,0:T(8,128)(2,1)} %tokens.1, bf16[128,3584]{1,0:T(8,128)(2,1)} %grad_out.1, s32[1,32]{1,0:T(1,128)} %bitcast.16, bf16[1,32]{1,0:T(2,128)(2,1)} %bitcast.18, ...), custom_call_target="tpu_custom_call" | custom-call | tf_op jit(solution)/shard_map/moe/pallas_call | solution.py:474
  101.9 2.7 %scatter.1 = (bf16[128,3584]{1,0:T(8,128)(2,1)}, f32[1,32]{1,0:T(1,128)}, bf16[224,768]{1,0:T(8,128)(2,1)}, bf16[224,768]{1,0:T(8,128)(2,1)}, bf16[224,768]{1,0:T(8,128)(2,1)}) custom-call(bf16[1,512,256]{2,1,0:T(8,128)(2,1)} %get-tuple-element.14.r4, s32[1,32]{1,0:T(1,128)} %bitcast.17, bf16[224,768]{1,0:T(8,128)(2,1)} %get-tuple-element.15.gwg, ...), custom_call_target="tpu_custom_call" | custom-call | tf_op jit(solution)/shard_map/scatter/pallas_call | solution.py:527

commit v3 on v2

--- a/solution.py
+++ b/solution.py
@@ -26,8 +26,8 @@
     cfg,
     tokens, grad_out, route, gates, wg, wu, wd,
     r4, gwg_out, gwu_out, gwd_out,
-    tok_v, dyo_v, wg_v, wu_v, wd_v, route_v, gates_v, wide, perm, a1, r1, a2, r2,
-    part, xa, arm_a, acc_a, arm_b, acc_b, xsend, xrecv, q_all, own_gg, a3, r3, a4, gw_v,
+    tok_v, dyo_v, wg_v, wu_v, wd_v, route_v, gates_v, wide, perm, a1, b1, r1, a2, r2, xd,
+    part, xa, arm_a, acc_a, arm_b, acc_b, xsend, xrecv, q_all, own_gg, grad_rows, a3, r3, a4, gw_v,
     load_sem, s1_sem, r1_sem, s2_sem, r2_sem, xas_sem, xar_sem, as_sem, ar_sem, xs_sem, xr_sem,
     qs_sem, qr_sem, qxs_sem, qxr_sem, s3_sem, r3_sem, s4_sem, r4_sem, out_sem,
 ):
@@ -38,6 +38,7 @@
     cap = n_ex
     hh = hid // 2
     win = width + 128
+    lanes = width // 2
 
     me = lax.axis_index("dp")
     ex = lax.axis_index("expert")
@@ -99,14 +100,16 @@
                 v = pltpu.roll(v, win - shift, 1)
             v = v[:, :width]
             pad = jnp.where(lane == piece, gate_own, 0.0) if q == 0 else 0.0
-            a1[q, d * n_ex:(d + 1) * n_ex, :] = jnp.where(lane < piece, v, pad).astype(BF16)
+            v = jnp.where(lane < piece, v, pad).astype(BF16)
+            for c in range(2):
+                a1[q, c, d * n_ex:(d + 1) * n_ex, :] = v[:, c * lanes:(c + 1) * lanes]
 
     class Exchange:
-        def __init__(self, axis, q, src, dst, send, recv):
+        def __init__(self, axis, q, c, src, dst, send, recv):
             self.axis = axis
             self.n, self.mine, self.size = (n_dp, me, n_ex) if axis == "dp" else (n_ex, ex, n_dp)
-            self.src, self.dst = src.at[q], dst.at[q]
-            self.send, self.recv = send.at[q], recv.at[q]
+            self.src, self.dst = src, dst.at[q, c]
+            self.send, self.recv = send.at[q, c], recv.at[q, c]
 
         def start(self):
             own = rows(self.mine, self.size)
@@ -132,24 +135,63 @@
             sent = self.src.at[pl.ds(0, (self.n - 1) * self.size)]
             pltpu.make_async_copy(sent, sent, self.send).wait()
 
-    ex1 = [Exchange("dp", q, a1, r1, s1_sem, r1_sem) for q in range(2)]
-    ex2 = [Exchange("expert", q, a2, r2, s2_sem, r2_sem) for q in range(2)]
-    ex3 = Exchange("expert", 0, a3, r3, s3_sem, r3_sem)
-    ex4 = Exchange("dp", 0, a4, r4, s4_sem, r4_sem)
-
-    gather(0, tok_v)
-    pl.semaphore_wait(barrier, n_dp + n_ex - 2)
-    ex1[0].start()
-    loads[3].wait()
-    gather(1, dyo_v)
-    ex1[1].start()
+    axes = ("dp", "expert")
+
+    def pair_of(q, first, second, r_first, r_second, sems):
+        return (
+            [Exchange(axes[c], q, c, first(c), r_first, *sems[:2]) for c in range(2)],
+            [Exchange(axes[1 - c], q, c, second(c), r_second, *sems[2:]) for c in range(2)],
+        )
+
+    def in_pair(q):
+        return pair_of(
+            q,
+            lambda c: b1.at[q] if c else a1.at[q, 0],
+            lambda c: a2.at[q, c],
+            r1, r2, (s1_sem, r1_sem, s2_sem, r2_sem),
+        )
+
+    ins = [in_pair(q) for q in range(2)]
+
+    def by_expert(v):
+        return dot(perm[...], v).astype(BF16)
+
+    def by_dp(v):
+        return dot(perm[...], v, 0, 0).astype(BF16)
+
+    def fetch(q, src):
+        gather(q, src)
+        b1[q] = by_expert(a1[q, 1])
+
     r_id = lax.broadcasted_iota(jnp.int32, (n_rows, n_rows), 0)
     c_id = lax.broadcasted_iota(jnp.int32, (n_rows, n_rows), 1)
-    perm[...] = jnp.where(c_id == lax.rem(r_id, n_dp) * n_ex + r_id // n_dp, 1.0, 0.0).astype(BF16)
+    bits = n_dp.bit_length() - 1
+    source = (r_id & (n_dp - 1)) * n_ex + lax.shift_right_logical(r_id, bits)
+    perm[...] = jnp.where(c_id == source, 1.0, 0.0).astype(BF16)
+    fetch(0, tok_v)
+    pl.semaphore_wait(barrier, n_dp + n_ex - 2)
+    for x in ins[0][0]:
+        x.start()
+    loads[3].wait()
+    fetch(1, dyo_v)
+    for x in ins[1][0]:
+        x.start()
     for q in range(2):
-        ex1[q].arrive()
-        a2[q] = dot(perm[...], r1[q]).astype(BF16)
-        ex2[q].start()
+        first, second = ins[q]
+        first[0].arrive()
+        a2[q, 0] = by_expert(r1[q, 0])
+        second[0].start()
+        first[1].arrive()
+        a2[q, 1] = by_dp(r1[q, 1])
+        second[1].start()
+
+    def settle(q):
+        second = ins[q][1]
+        second[0].arrive()
+        xd[q, :, :lanes] = r2[q, 0]
+        second[1].arrive()
+        xd[q, :, lanes:] = by_expert(r2[q, 1])
+
     for load in loads[4:]:
         load.wait()
 
@@ -247,17 +289,17 @@
 
     last = ny // 2
 
-    ex2[0].arrive()
-    partial(0, dot(r2[0, :, :piece], wg_v[...]))
+    settle(0)
+    partial(0, dot(xd[0, :, :piece], wg_v[...]))
     xa_send(0)
     hop(0, 1, 0)
-    partial(1, dot(r2[0, :, :piece], wu_v[...]))
+    partial(1, dot(xd[0, :, :piece], wu_v[...]))
     xa_send(1)
     hop(1, 1, 0)
     hop(0, 0, 0)
     hop(0, 1, 1)
-    ex2[1].arrive()
-    partial(2, dot(r2[1, :, :piece], wd_v[...]))
+    settle(1)
+    partial(2, dot(xd[1, :, :piece], wd_v[...]))
     xa_send(2)
     hop(2, 1, 0)
     for h in range(1, last + 2):
@@ -270,7 +312,7 @@
                 b_end(m)
     gate_pre = finish(0)
     up_pre = finish(1)
-    gate_rows = r2[0, rows(me, cap), :].astype(F32)
+    gate_rows = xd[0, rows(me, cap), :].astype(F32)
     wl = lax.broadcasted_iota(jnp.int32, (cap, width), 1)
     gate_w = jnp.sum(jnp.where(wl == piece, gate_rows, 0.0), axis=1, keepdims=True)
     sig = 1.0 / (1.0 + jnp.exp(-gate_pre))
@@ -329,20 +371,15 @@
     keep(2, grad_hidden * act)
     q_xb(2).start()
     q_hop(2, 0, 0)
-    keep(0, gate_w * hidden)
-    q_xb(0).start()
-    own_gg[...] = jnp.broadcast_to(jnp.sum(hidden * base, axis=1, keepdims=True), own_gg.shape)
     q_hop(1, 1, 0)
     q_hop(2, 1, 0)
-    q_hop(0, 0, 0)
+    keep(0, gate_w * hidden)
+    own_gg[...] = jnp.broadcast_to(jnp.sum(hidden * base, axis=1, keepdims=True), own_gg.shape)
     for h in range(1, last + 1):
-        q_hop(1, 0, h)
-        q_hop(1, 1, h)
-        q_hop(2, 0, h)
-        q_hop(2, 1, h)
-        q_hop(0, 1, h - 1)
-        if h < last:
-            q_hop(0, 0, h)
+        for m in (1, 2):
+            q_hop(m, 0, h)
+            q_hop(m, 1, h)
+    q_xb(0).start()
     q_end(1)
     q_end(2)
 
@@ -351,38 +388,62 @@
             [q_all[m, c].reshape(n_rows, hh) for c in range(2)], axis=1
         )
 
-    a3[0, :, width - 128:] = jnp.zeros((n_rows, 128), BF16)
-    a3[0, :, :piece] = (dot(back(1), wg_v[...], 1, 1) + dot(back(2), wu_v[...], 1, 1)).astype(BF16)
-    tail = a3[0, rows(me, cap), width - 128:].astype(F32)
+    grad_rows[:, width - 128:] = jnp.zeros((n_rows, 128), BF16)
+    grad_rows[:, :piece] = (
+        dot(back(1), wg_v[...], 1, 1) + dot(back(2), wu_v[...], 1, 1)
+    ).astype(BF16)
+    tail = grad_rows[rows(me, cap), width - 128:].astype(F32)
     tl = lax.broadcasted_iota(jnp.int32, tail.shape, 1) + (width - 128)
     rest = own_gg[...]
     for n in range(3):
         top = rest.astype(BF16).astype(F32)
         tail = jnp.where(tl == piece + n, top, tail)
         rest = rest - top
-    a3[0, rows(me, cap), width - 128:] = tail.astype(BF16)
-    ex3.start()
-
-    q_hop(0, 0, last)
-    q_hop(0, 1, last)
+    grad_rows[rows(me, cap), width - 128:] = tail.astype(BF16)
+
+    home = [
+        Exchange("expert", 0, 0, a3.at[0], r3, s3_sem, r3_sem),
+        Exchange("dp", 0, 1, a3.at[1], r3, s3_sem, r3_sem),
+    ]
+    home2 = [
+        Exchange("dp", 0, 0, a4.at[0], r4, s4_sem, r4_sem),
+        Exchange("expert", 0, 1, a4.at[1], r4, s4_sem, r4_sem),
+    ]
+    a3[0] = grad_rows[:, :lanes]
+    home[0].start()
+    a3[1] = by_dp(grad_rows[:, lanes:])
+    home[1].start()
+
     outs = [
         pltpu.make_async_copy(gw_v.at[m], dst, out_sem.at[m])
         for m, dst in ((1, gwg_out), (2, gwu_out), (0, gwd_out))
     ]
-    gw_v[1] = dot(r2[0, :, :piece], back(1), 0, 0).astype(BF16)
+    q_hop(0, 0, 0)
+    q_hop(0, 1, 0)
+    gw_v[1] = dot(xd[0, :, :piece], back(1), 0, 0).astype(BF16)
     outs[0].start()
-    gw_v[2] = dot(r2[0, :, :piece], back(2), 0, 0).astype(BF16)
+    q_hop(0, 0, 1)
+    q_hop(0, 1, 1)
+    gw_v[2] = dot(xd[0, :, :piece], back(2), 0, 0).astype(BF16)
     outs[1].start()
-
-    ex3.arrive()
-    a4[0] = dot(perm[...], r3[0], 0, 0).astype(BF16)
-    ex4.start()
+    for h in range(2, last):
+        q_hop(0, 0, h)
+        q_hop(0, 1, h)
+    home[0].arrive()
+    a4[0] = by_dp(r3[0, 0])
+    home2[0].start()
+    home[1].arrive()
+    a4[1] = by_expert(r3[0, 1])
+    home2[1].start()
+    q_hop(0, 0, last)
+    q_hop(0, 1, last)
     q_end(0)
-    gw_v[0] = dot(r2[1, :, :piece], back(0), 0, 0).astype(BF16)
+    gw_v[0] = dot(xd[1, :, :piece], back(0), 0, 0).astype(BF16)
     outs[2].start()
-    ex4.arrive()
-
-    for x in (*ex1, *ex2, ex3, ex4):
+    for x in home2:
+        x.arrive()
+
+    for x in (*ins[0][0], *ins[0][1], *ins[1][0], *ins[1][1], *home, *home2):
         x.drain()
 
     def sent(ref, sem):
@@ -402,7 +463,7 @@
 
 def last_kernel(
     cfg, r4, route, gwg, gwu, gwd, gt_out, gg_out, gwg_out, gwu_out, gwd_out,
-    r4_v, route_v, gw_v, wide, gt_v, gg_v, in_sem, out_sem,
+    r4_v, late, route_v, gw_v, wide, gt_v, gg_v, in_sem, out_sem,
 ):
     n_dp, n_ex, piece, width, hid = cfg
     d_model = n_dp * piece
@@ -426,12 +487,19 @@
     wide[...] = jnp.zeros(wide.shape, F32)
     ins[0].wait()
     ins[1].wait()
+    late[...] = r4_v[0, 1].astype(F32)
     lane = lax.broadcasted_iota(jnp.int32, (n_ex, width), 1)
     sums = jnp.zeros((n_ex, width), F32)
     for d in range(n_dp):
         start = (piece * d) // 128 * 128
         shift = piece * d - start
-        v = r4_v[0, d * n_ex:(d + 1) * n_ex, :].astype(F32)
+        v = jnp.concatenate(
+            [
+                r4_v[0, 0, d * n_ex:(d + 1) * n_ex, :].astype(F32),
+                late[pl.ds(d, n_ex, stride=n_dp), :],
+            ],
+            axis=1,
+        )
         sums = sums + jnp.where((lane >= piece) & (lane < piece + 3), v, 0.0)
         v = jnp.concatenate([jnp.where(lane < piece, v, 0.0), jnp.zeros((n_ex, 128), F32)], axis=1)
         if shift:
@@ -469,11 +537,13 @@
     weights = jax.ShapeDtypeStruct((piece, hid), BF16)
     route_row = route.reshape(1, n_ex)
     wide = pltpu.VMEM((n_ex, d_model + width + 128), F32)
-    block = pltpu.VMEM((2, n_rows, width), BF16)
-    one_block = pltpu.VMEM((1, n_rows, width), BF16)
+    lanes = width // 2
+    whole = pltpu.VMEM((2, n_rows, width), BF16)
+    block = pltpu.VMEM((2, 2, n_rows, lanes), BF16)
+    halves = pltpu.VMEM((2, n_rows, lanes), BF16)
     r4, gwg, gwu, gwd = pl.pallas_call(
         functools.partial(kernel, cfg),
-        out_shape=(jax.ShapeDtypeStruct((1, n_rows, width), BF16), weights, weights, weights),
+        out_shape=(jax.ShapeDtypeStruct((1, 2, n_rows, lanes), BF16), weights, weights, weights),
         in_specs=[any_spec] * 7,
         out_specs=(any_spec,) * 4,
         scratch_shapes=[
@@ -486,7 +556,7 @@
             pltpu.VMEM((1, n_ex), BF16),
             wide,
             pltpu.VMEM((n_rows, n_rows), BF16),
-            block, block, block, block,
+            block, halves, block, block, block, whole,
             pltpu.VMEM((3, 2, NX, ny, cap, hh), BF16),
             pltpu.VMEM((3, ny, cap, hh), BF16),
             pltpu.VMEM((3, 2, hops, cap, hh), BF16),
@@ -497,18 +567,21 @@
             pltpu.VMEM((3, cap, hh), BF16),
             pltpu.VMEM((3, 2, NX, ny, cap, hh), BF16),
             pltpu.VMEM((cap, 128), F32),
-            one_block, one_block, one_block,
+            pltpu.VMEM((n_rows, width), BF16),
+            halves,
+            pltpu.VMEM((1, 2, n_rows, lanes), BF16),
+            halves,
             pltpu.VMEM((3, piece, hid), BF16),
             dma((7,)),
-            dma((2,)), dma((2,)),
-            dma((2,)), dma((2,)),
+            dma((2, 2)), dma((2, 2)),
+            dma((2, 2)), dma((2, 2)),
             dma((1,)), dma((3, ny)),
             dma((2,)), dma((3, 2, 2, hops)),
             dma((1,)), dma((3,)),
             dma((2,)), dma((3, 2, 2, hops)),
             dma((2,)), dma((3, 2)),
-            dma((1,)), dma((1,)),
-            dma((1,)), dma((1,)),
+            dma((1, 2)), dma((1, 2)),
+            dma((1, 2)), dma((1, 2)),
             dma((3,)),
         ],
         compiler_params=pltpu.CompilerParams(
@@ -534,7 +607,8 @@
         in_specs=[any_spec] * 5,
         out_specs=(any_spec,) * 5,
         scratch_shapes=[
-            pltpu.VMEM((1, n_rows, width), BF16),
+            pltpu.VMEM((1, 2, n_rows, lanes), BF16),
+            pltpu.VMEM((n_rows, lanes), F32),
             pltpu.VMEM((1, n_ex), jnp.int32),
             pltpu.VMEM((3, piece, hid), BF16),
             wide,

time: 105 us -> 106 us (level)
  no operation moved by 1% of the time
where the time goes in v3:
time: 106 us; the launch traced here: 105 us
  Pallas kernels  105 us (99%)
    pallas_call x1, Pallas kernels, local(): pl.pallas_call(functools.partial(kernel, cfg), out_shape=(jax.ShapeDtypeS...  102 us
    pallas_call x1, Pallas kernels, local(): pl.pallas_call(functools.partial(last_kernel, cfg), out_shape=(jax.ShapeD...  2.67 us

profile of v3, /device:TPU:1, one launch (start us, length us, event | category | flops | bytes accessed | tf_op | source)
XLA Modules:
  0.0 105.4 jit_solution(2592553286185092100)
XLA Ops:
  0.6 102.1 %moe.1 = (bf16[1,2,512,128]{3,2,1,0:T(8,128)(2,1)}, bf16[224,768]{1,0:T(8,128)(2,1)}, bf16[224,768]{1,0:T(8,128)(2,1)}, bf16[224,768]{1,0:T(8,128)(2,1)}) custom-call(bf16[128,3584]{1,0:T(8,128)(2,1)} %tokens.1, bf16[128,3584]{1,0:T(8,128)(2,1)} %grad_out.1, s32[1,32]{1,0:T(1,128)} %bitcast.16, bf16[1,32]{1,0:T(2,128)(2,1)} %bitcast.18, ...), custom_call_target="tpu_custom_call" | custom-call | tf_op jit(solution)/shard_map/moe/pallas_call | solution.py:544
  102.7 2.7 %scatter.1 = (bf16[128,3584]{1,0:T(8,128)(2,1)}, f32[1,32]{1,0:T(1,128)}, bf16[224,768]{1,0:T(8,128)(2,1)}, bf16[224,768]{1,0:T(8,128)(2,1)}, bf16[224,768]{1,0:T(8,128)(2,1)}) custom-call(bf16[1,2,512,128]{3,2,1,0:T(8,128)(2,1)} %get-tuple-element.14.r4, s32[1,32]{1,0:T(1,128)} %bitcast.17, bf16[224,768]{1,0:T(8,128)(2,1)} %get-tuple-element.15.gwg, ...), custom_call_target="tpu_custom_call" | custom-call | tf_op jit(solution)/shard_map/scatter/pallas_call | solution.py:600

commit v4 on v3

--- a/solution.py
+++ b/solution.py
@@ -216,10 +216,10 @@
             device_id={"dp": pair},
         )
 
-    far_first = sorted(range(-(ny // 2) + 1, ny // 2 + 1), key=lambda o: -abs(o))
-
-    def xa_send(m):
-        for off in far_first:
+    def xa_send(m, level):
+        long = sign(m % 2)
+        n = ny // 2 - level
+        for off in {1: (long,), 0: (0,)}.get(n, (n * long, (1 - n) * long)):
             xa_copy(m, off).start()
 
     def arm_copy(m, c, s, h):
@@ -277,55 +277,64 @@
         xsend[m] = b_total(m, 1 - xl).astype(BF16)
         x_copy(m).start()
 
-    def finish(m):
+    def end_a(m):
         xa_copy(m, 0).wait_recv()
         v = part[m, 0, xl, y].astype(F32) + xa[m, y].astype(F32)
         for s in range(2):
             n = arm_len(m, 0, s)
             arm_copy(m, 0, s, n - 1).wait_recv()
             v = v + arm_a[m, s, n - 1].astype(F32)
+        return v
+
+    def end_b(m):
         x_copy(m).wait_recv()
-        return jnp.concatenate([v, b_total(m, xl) + xrecv[m].astype(F32)], axis=1)
+        return b_total(m, xl) + xrecv[m].astype(F32)
 
     last = ny // 2
 
     settle(0)
     partial(0, dot(xd[0, :, :piece], wg_v[...]))
-    xa_send(0)
     hop(0, 1, 0)
+    xa_send(0, 0)
     partial(1, dot(xd[0, :, :piece], wu_v[...]))
-    xa_send(1)
     hop(1, 1, 0)
-    hop(0, 0, 0)
-    hop(0, 1, 1)
+    xa_send(1, 0)
+    xa_send(0, 1)
+    xa_send(1, 1)
     settle(1)
     partial(2, dot(xd[1, :, :piece], wd_v[...]))
-    xa_send(2)
     hop(2, 1, 0)
-    for h in range(1, last + 2):
-        for m, c, k in (
-            (1, 1, h), (1, 0, h - 1), (0, 0, h), (0, 1, h + 1), (2, 1, h), (2, 0, h - 1)
-        ):
-            if k < last:
-                hop(m, c, k)
-            elif k == last and c == 1:
+    xa_send(2, 0)
+    xa_send(2, 1)
+    for level in range(2, last + 1):
+        for m in range(3):
+            xa_send(m, level)
+    for h in range(1, last + 1):
+        for m in range(3):
+            if h < last:
+                hop(m, 1, h)
+            else:
                 b_end(m)
-    gate_pre = finish(0)
-    up_pre = finish(1)
+        for m in range(3):
+            hop(m, 0, h - 1)
+
     gate_rows = xd[0, rows(me, cap), :].astype(F32)
     wl = lax.broadcasted_iota(jnp.int32, (cap, width), 1)
     gate_w = jnp.sum(jnp.where(wl == piece, gate_rows, 0.0), axis=1, keepdims=True)
-    sig = 1.0 / (1.0 + jnp.exp(-gate_pre))
-    act = gate_pre * sig
-    hidden = act * up_pre
-    slope = up_pre * sig * (1.0 + gate_pre * (1.0 - sig))
-    base = finish(2)
-    grad_hidden = gate_w * base
-
-    def keep(m, value):
-        value = value.astype(BF16)
-        for c in range(2):
-            q_all[m, c, xl, y] = value[:, c * hh:(c + 1) * hh]
+
+    def activate(c, end):
+        gate_pre = end(0)
+        up_pre = end(1)
+        sig = 1.0 / (1.0 + jnp.exp(-gate_pre))
+        act = gate_pre * sig
+        hidden = act * up_pre
+        slope = up_pre * sig * (1.0 + gate_pre * (1.0 - sig))
+        base = end(2)
+        grad_hidden = gate_w * base
+        q_all[1, c, xl, y] = (grad_hidden * slope).astype(BF16)
+        q_all[2, c, xl, y] = (grad_hidden * act).astype(BF16)
+        q_all[0, c, xl, y] = (gate_w * hidden).astype(BF16)
+        return jnp.sum(hidden * base, axis=1, keepdims=True)
 
     def q_remote(block, send, recv, device):
         return pltpu.make_async_remote_copy(
@@ -365,21 +374,18 @@
         side = q_all.at[m, 0, 1 - xl]
         pltpu.make_async_copy(side, side, qxr_sem.at[m, 0]).wait()
 
-    keep(1, grad_hidden * slope)
-    q_xb(1).start()
-    q_hop(1, 0, 0)
-    keep(2, grad_hidden * act)
-    q_xb(2).start()
-    q_hop(2, 0, 0)
-    q_hop(1, 1, 0)
-    q_hop(2, 1, 0)
-    keep(0, gate_w * hidden)
-    own_gg[...] = jnp.broadcast_to(jnp.sum(hidden * base, axis=1, keepdims=True), own_gg.shape)
+    gg = activate(1, end_b)
+    for m in (1, 2, 0):
+        q_xb(m).start()
+    gg = gg + activate(0, end_a)
+    own_gg[...] = jnp.broadcast_to(gg, own_gg.shape)
+    for m in (1, 2):
+        q_hop(m, 1, 0)
+        q_hop(m, 0, 0)
     for h in range(1, last + 1):
-        for m in (1, 2):
-            q_hop(m, 0, h)
-            q_hop(m, 1, h)
-    q_xb(0).start()
+        for m, k in ((1, h), (2, h), (0, h - 1)):
+            q_hop(m, 1, k)
+            q_hop(m, 0, k)
     q_end(1)
     q_end(2)
 
@@ -418,25 +424,18 @@
         pltpu.make_async_copy(gw_v.at[m], dst, out_sem.at[m])
         for m, dst in ((1, gwg_out), (2, gwu_out), (0, gwd_out))
     ]
-    q_hop(0, 0, 0)
-    q_hop(0, 1, 0)
+    q_hop(0, 1, last)
+    q_hop(0, 0, last)
     gw_v[1] = dot(xd[0, :, :piece], back(1), 0, 0).astype(BF16)
     outs[0].start()
-    q_hop(0, 0, 1)
-    q_hop(0, 1, 1)
     gw_v[2] = dot(xd[0, :, :piece], back(2), 0, 0).astype(BF16)
     outs[1].start()
-    for h in range(2, last):
-        q_hop(0, 0, h)
-        q_hop(0, 1, h)
     home[0].arrive()
     a4[0] = by_dp(r3[0, 0])
     home2[0].start()
     home[1].arrive()
     a4[1] = by_expert(r3[0, 1])
     home2[1].start()
-    q_hop(0, 0, last)
-    q_hop(0, 1, last)
     q_end(0)
     gw_v[0] = dot(xd[1, :, :piece], back(0), 0, 0).astype(BF16)
     outs[2].start()

time: 106 us -> 97.1 us (0.916)
  Pallas kernels: 105 us -> 96.3 us
    pallas_call x1, Pallas kernels: 102 us -> 93.6 us  [local(): pl.pallas_call(functools.partial(kernel, cfg), out_shape=(jax.ShapeDtypeS...]
where the time goes in v4:
time: 97.1 us; the launch traced here: 96.9 us
  Pallas kernels  96.3 us (99%)
    pallas_call x1, Pallas kernels, local(): pl.pallas_call(functools.partial(kernel, cfg), out_shape=(jax.ShapeDtypeS...  93.6 us
    pallas_call x1, Pallas kernels, local(): pl.pallas_call(functools.partial(last_kernel, cfg), out_shape=(jax.ShapeD...  2.67 us

profile of v4, /device:TPU:1, one launch (start us, length us, event | category | flops | bytes accessed | tf_op | source)
XLA Modules:
  0.0 96.9 jit_solution(15169632503291797870)
XLA Ops:
  0.6 93.6 %moe.1 = (bf16[1,2,512,128]{3,2,1,0:T(8,128)(2,1)}, bf16[224,768]{1,0:T(8,128)(2,1)}, bf16[224,768]{1,0:T(8,128)(2,1)}, bf16[224,768]{1,0:T(8,128)(2,1)}) custom-call(bf16[128,3584]{1,0:T(8,128)(2,1)} %tokens.1, bf16[128,3584]{1,0:T(8,128)(2,1)} %grad_out.1, s32[1,32]{1,0:T(1,128)} %bitcast.16, bf16[1,32]{1,0:T(2,128)(2,1)} %bitcast.18, ...), custom_call_target="tpu_custom_call" | custom-call | tf_op jit(solution)/shard_map/moe/pallas_call | solution.py:543
  94.3 2.7 %scatter.1 = (bf16[128,3584]{1,0:T(8,128)(2,1)}, f32[1,32]{1,0:T(1,128)}, bf16[224,768]{1,0:T(8,128)(2,1)}, bf16[224,768]{1,0:T(8,128)(2,1)}, bf16[224,768]{1,0:T(8,128)(2,1)}) custom-call(bf16[1,2,512,128]{3,2,1,0:T(8,128)(2,1)} %get-tuple-element.14.r4, s32[1,32]{1,0:T(1,128)} %bitcast.17, bf16[224,768]{1,0:T(8,128)(2,1)} %get-tuple-element.15.gwg, ...), custom_call_target="tpu_custom_call" | custom-call | tf_op jit(solution)/shard_map/scatter/pallas_call | solution.py:599

commit v5 on v4

--- a/solution.py
+++ b/solution.py
@@ -82,6 +82,11 @@
 
     lane = lax.broadcasted_iota(jnp.int32, (n_ex, width), 1)
     wide[:, d_model:] = jnp.zeros((n_ex, wide.shape[1] - d_model), F32)
+    r_id = lax.broadcasted_iota(jnp.int32, (n_rows, n_rows), 0)
+    c_id = lax.broadcasted_iota(jnp.int32, (n_rows, n_rows), 1)
+    bits = n_dp.bit_length() - 1
+    source = (r_id & (n_dp - 1)) * n_ex + lax.shift_right_logical(r_id, bits)
+    perm[...] = jnp.where(c_id == source, 1.0, 0.0).astype(BF16)
     for load in loads[:3]:
         load.wait()
     pick = one_hot_rows(route_v[...], tok_v.shape[0])
@@ -159,23 +164,15 @@
     def by_dp(v):
         return dot(perm[...], v, 0, 0).astype(BF16)
 
-    def fetch(q, src):
+    for q, src in enumerate((tok_v, dyo_v)):
+        if q == 1:
+            loads[3].wait()
         gather(q, src)
+        if q == 0:
+            pl.semaphore_wait(barrier, n_dp + n_ex - 2)
+        ins[q][0][0].start()
         b1[q] = by_expert(a1[q, 1])
-
-    r_id = lax.broadcasted_iota(jnp.int32, (n_rows, n_rows), 0)
-    c_id = lax.broadcasted_iota(jnp.int32, (n_rows, n_rows), 1)
-    bits = n_dp.bit_length() - 1
-    source = (r_id & (n_dp - 1)) * n_ex + lax.shift_right_logical(r_id, bits)
-    perm[...] = jnp.where(c_id == source, 1.0, 0.0).astype(BF16)
-    fetch(0, tok_v)
-    pl.semaphore_wait(barrier, n_dp + n_ex - 2)
-    for x in ins[0][0]:
-        x.start()
-    loads[3].wait()
-    fetch(1, dyo_v)
-    for x in ins[1][0]:
-        x.start()
+        ins[q][0][1].start()
     for q in range(2):
         first, second = ins[q]
         first[0].arrive()
@@ -313,10 +310,11 @@
         for m in range(3):
             if h < last:
                 hop(m, 1, h)
-            else:
+            elif h == last:
                 b_end(m)
-        for m in range(3):
-            hop(m, 0, h - 1)
+        if h >= 1:
+            for m in range(3):
+                hop(m, 0, h - 1)
 
     gate_rows = xd[0, rows(me, cap), :].astype(F32)
     wl = lax.broadcasted_iota(jnp.int32, (cap, width), 1)
@@ -383,29 +381,19 @@
         q_hop(m, 1, 0)
         q_hop(m, 0, 0)
     for h in range(1, last + 1):
-        for m, k in ((1, h), (2, h), (0, h - 1)):
-            q_hop(m, 1, k)
-            q_hop(m, 0, k)
+        for m, k in ((1, h), (2, h), (0, h - 2)):
+            if m > 0 or 0 <= k < last - 2:
+                q_hop(m, 0, k)
+                q_hop(m, 1, k)
     q_end(1)
-    q_end(2)
 
     def back(m):
         return jnp.concatenate(
             [q_all[m, c].reshape(n_rows, hh) for c in range(2)], axis=1
         )
 
-    grad_rows[:, width - 128:] = jnp.zeros((n_rows, 128), BF16)
-    grad_rows[:, :piece] = (
-        dot(back(1), wg_v[...], 1, 1) + dot(back(2), wu_v[...], 1, 1)
-    ).astype(BF16)
-    tail = grad_rows[rows(me, cap), width - 128:].astype(F32)
-    tl = lax.broadcasted_iota(jnp.int32, tail.shape, 1) + (width - 128)
-    rest = own_gg[...]
-    for n in range(3):
-        top = rest.astype(BF16).astype(F32)
-        tail = jnp.where(tl == piece + n, top, tail)
-        rest = rest - top
-    grad_rows[rows(me, cap), width - 128:] = tail.astype(BF16)
+    def rows_grad(m, w, lo, hi):
+        return dot(back(m), w[lo:hi, :], 1, 1)
 
     home = [
         Exchange("expert", 0, 0, a3.at[0], r3, s3_sem, r3_sem),
@@ -415,19 +403,36 @@
         Exchange("dp", 0, 0, a4.at[0], r4, s4_sem, r4_sem),
         Exchange("expert", 0, 1, a4.at[1], r4, s4_sem, r4_sem),
     ]
-    a3[0] = grad_rows[:, :lanes]
+    gate_part = rows_grad(1, wg_v, 0, lanes)
+    q_end(2)
+    a3[0] = (gate_part + rows_grad(2, wu_v, 0, lanes)).astype(BF16)
     home[0].start()
-    a3[1] = by_dp(grad_rows[:, lanes:])
+    grad_rows[...] = jnp.zeros((n_rows, lanes), BF16)
+    grad_rows[:, :piece - lanes] = (
+        rows_grad(1, wg_v, lanes, piece) + rows_grad(2, wu_v, lanes, piece)
+    ).astype(BF16)
+    tail = grad_rows[rows(me, cap), :].astype(F32)
+    tl = lax.broadcasted_iota(jnp.int32, tail.shape, 1) + lanes
+    rest = own_gg[...]
+    for n in range(3):
+        top = rest.astype(BF16).astype(F32)
+        tail = jnp.where(tl == piece + n, top, tail)
+        rest = rest - top
+    grad_rows[rows(me, cap), :] = tail.astype(BF16)
+
+    a3[1] = by_dp(grad_rows[...])
     home[1].start()
 
     outs = [
         pltpu.make_async_copy(gw_v.at[m], dst, out_sem.at[m])
         for m, dst in ((1, gwg_out), (2, gwu_out), (0, gwd_out))
     ]
-    q_hop(0, 1, last)
-    q_hop(0, 0, last)
+    q_hop(0, 1, last - 2)
+    q_hop(0, 0, last - 2)
     gw_v[1] = dot(xd[0, :, :piece], back(1), 0, 0).astype(BF16)
     outs[0].start()
+    q_hop(0, 1, last - 1)
+    q_hop(0, 0, last - 1)
     gw_v[2] = dot(xd[0, :, :piece], back(2), 0, 0).astype(BF16)
     outs[1].start()
     home[0].arrive()
@@ -436,6 +441,8 @@
     home[1].arrive()
     a4[1] = by_expert(r3[0, 1])
     home2[1].start()
+    q_hop(0, 1, last)
+    q_hop(0, 0, last)
     q_end(0)
     gw_v[0] = dot(xd[1, :, :piece], back(0), 0, 0).astype(BF16)
     outs[2].start()
@@ -467,6 +474,8 @@
     n_dp, n_ex, piece, width, hid = cfg
     d_model = n_dp * piece
     win = width + 128
+    step = d_model // 4
+    parts = [pl.ds(n * step, step) for n in range(4)]
     ins = [
         pltpu.make_async_copy(src, dst, in_sem.at[n])
         for n, (src, dst) in enumerate(
@@ -478,7 +487,8 @@
         pltpu.make_async_copy(src, dst, out_sem.at[n])
         for n, (src, dst) in enumerate(
             [(gw_v.at[m], dst) for m, dst in enumerate((gwg_out, gwu_out, gwd_out))]
-            + [(gg_v, gg_out), (gt_v, gt_out)]
+            + [(gg_v, gg_out)]
+            + [(gt_v.at[:, part], gt_out.at[:, part]) for part in parts]
         )
     ]
     for copy in ins:
@@ -513,8 +523,10 @@
     gg_v[...] = jnp.sum(jnp.where(e_row == e_col, column, 0.0), axis=0, keepdims=True)
     outs[3].start()
     pick = one_hot_rows(route_v[...], gt_v.shape[0])
-    gt_v[...] = dot(pick, wide[:, :d_model].astype(BF16)).astype(BF16)
-    outs[4].start()
+    for n in range(4):
+        cut = slice(n * step, (n + 1) * step)
+        gt_v[:, cut] = dot(pick, wide[:, cut].astype(BF16)).astype(BF16)
+        outs[4 + n].start()
     for copy in outs:
         copy.wait()
 
@@ -566,7 +578,7 @@
             pltpu.VMEM((3, cap, hh), BF16),
             pltpu.VMEM((3, 2, NX, ny, cap, hh), BF16),
             pltpu.VMEM((cap, 128), F32),
-            pltpu.VMEM((n_rows, width), BF16),
+            pltpu.VMEM((n_rows, lanes), BF16),
             halves,
             pltpu.VMEM((1, 2, n_rows, lanes), BF16),
             halves,
@@ -614,7 +626,7 @@
             pltpu.VMEM((tok_dev, d_model), BF16),
             pltpu.VMEM((1, n_ex), F32),
             dma((5,)),
-            dma((5,)),
+            dma((8,)),
         ],
         compiler_params=pltpu.CompilerParams(vmem_limit_bytes=56 * 1024 * 1024),
         name="scatter",

time: 97.1 us -> 96.5 us (level)
  no operation moved by 1% of the time
where the time goes in v5:
time: 96.5 us; the launch traced here: 96.4 us
  Pallas kernels  95.7 us (99%)
    pallas_call x1, Pallas kernels, local(): pl.pallas_call(functools.partial(kernel, cfg), out_shape=(jax.ShapeDtypeS...  93.2 us
    pallas_call x1, Pallas kernels, local(): pl.pallas_call(functools.partial(last_kernel, cfg), out_shape=(jax.ShapeD...  2.52 us

profile of v5, /device:TPU:1, one launch (start us, length us, event | category | flops | bytes accessed | tf_op | source)
XLA Modules:
  0.0 96.4 jit_solution(9897796472665492485)
XLA Ops:
  0.6 93.2 %moe.1 = (bf16[1,2,512,128]{3,2,1,0:T(8,128)(2,1)}, bf16[224,768]{1,0:T(8,128)(2,1)}, bf16[224,768]{1,0:T(8,128)(2,1)}, bf16[224,768]{1,0:T(8,128)(2,1)}) custom-call(bf16[128,3584]{1,0:T(8,128)(2,1)} %tokens.1, bf16[128,3584]{1,0:T(8,128)(2,1)} %grad_out.1, s32[1,32]{1,0:T(1,128)} %bitcast.16, bf16[1,32]{1,0:T(2,128)(2,1)} %bitcast.18, ...), custom_call_target="tpu_custom_call" | custom-call | tf_op jit(solution)/shard_map/moe/pallas_call | solution.py:555
  93.8 2.5 %scatter.1 = (bf16[128,3584]{1,0:T(8,128)(2,1)}, f32[1,32]{1,0:T(1,128)}, bf16[224,768]{1,0:T(8,128)(2,1)}, bf16[224,768]{1,0:T(8,128)(2,1)}, bf16[224,768]{1,0:T(8,128)(2,1)}) custom-call(bf16[1,2,512,128]{3,2,1,0:T(8,128)(2,1)} %get-tuple-element.14.r4, s32[1,32]{1,0:T(1,128)} %bitcast.17, bf16[224,768]{1,0:T(8,128)(2,1)} %get-tuple-element.15.gwg, ...), custom_call_target="tpu_custom_call" | custom-call | tf_op jit(solution)/shard_map/scatter/pallas_call | solution.py:611
